TPU v7x, 512 devices: a whole 4x4x16 slice. The times are simulated.
512 devices in a mesh: grp: 16 (over x, y), dev: 32 (over z, core).
Axes of the slice: x: 4, y: 4, z: 16, core: 2. Of those that a mesh axis runs over, the one named last changes fastest.
Arguments:
- rhs: float32 [16, 524288], P(None, ('grp', 'dev')), may hold values from -6 to 6
- leaf_basis: float32 [64, 524288], P(None, ('grp', 'dev'))
- near_blocks: float32 [64, 1048576], P(None, ('grp', 'dev')), may hold values from -0.75 to 0.75
- near_partner: int32 [8192], P(('grp', 'dev')), may hold values from 0 to 8191, as said below
- local_transfer: float32 [64, 983040], P(None, ('grp', 'dev'))
- local_coupling: float32 [64, 983040], P(None, ('grp', 'dev')), may hold values from -0.75 to 0.75
- far_partner: int32 [512, 30], P(('grp', 'dev')), may hold values from 0 to 8191, as said below
- dev_transfer: float32 [16, 64, 3968], P('grp')
- dev_coupling: float32 [16, 64, 3968], P('grp'), may hold values from -4 to 4
- grp_transfer: float32 [64, 1920], replicated
- grp_coupling: float32 [64, 1920], replicated, may hold values from -6 to 6
Outputs:
- product: float32 [16, 524288], P(None, ('grp', 'dev'))
- root_factor: float32 [64, 64], replicated
Inputs may be any that keep to these rules, and one draw needn't show every extreme that they name: near_partner[l] is a leaf other than l, at most 16 leaves away; some leaf's partner is exactly 16 leaves away. `far_partner`: in row s, entry 2 * 16 - 2 * m + j (m = 16 >> k, level k, 0 <= j < m) names a node of level k other than node s * m + j and at most m nodes from it; at every level some entry is exactly m nodes away.
All inputs are finite; a program needn't handle non-finite values.
Results may differ from a plain program's by a relative error of at most 0.0001.
Values sent between devices are 32-bit elements; how exact they have to be, the bound alone decides.
A program may use at most 64 MiB of HBM per device.

v0:
```python
import jax
import jax.numpy as jnp
from jax import lax
from jax.sharding import PartitionSpec as P

RANK = 64
LEAF = 64
NRHS = 16
LOC = 4
LEAF_DEV = 16
LOCAL_NODES = 30


precise = lax.Precision.HIGHEST


def with_halo(cells, sides, width):
    for axis, dim in sides:
        count = lax.axis_size(axis)
        ends = count - 1
        head = lax.slice_in_dim(cells, 0, width, axis=dim)
        tail = lax.slice_in_dim(cells, cells.shape[dim] - width, cells.shape[dim], axis=dim)
        cells = jnp.concatenate(
            [
                lax.ppermute(tail, axis, [(i, (i + 1) % count) for i in range(ends)]),
                cells,
                lax.ppermute(head, axis, [((i + 1) % count, i) for i in range(ends)]),
            ],
            axis=dim,
        )
    return cells


def partner(array, axis, bit):
    return lax.ppermute(array, axis, [(i, i ^ 1 << bit) for i in range(lax.axis_size(axis))])


def blocks_of(matrix, node_count):
    return matrix.reshape(matrix.shape[0], node_count, -1).transpose(1, 0, 2)


def invert_lower(factor):
    identity = jnp.broadcast_to(jnp.eye(factor.shape[-1], dtype=jnp.float32), factor.shape)
    return jax.scipy.linalg.solve_triangular(factor, identity, lower=True)


def combine(factors, projected, transfers):
    upper_blocks = jnp.einsum("nji,njk->nik", factors, transfers, precision=precise)
    even_upper = upper_blocks[0::2]
    odd_upper = upper_blocks[1::2]
    gram_matrix = jnp.einsum(
        "nji,njk->nik", even_upper, even_upper, precision=precise
    ) + jnp.einsum("nji,njk->nik", odd_upper, odd_upper, precision=precise)
    parent = jnp.linalg.cholesky(gram_matrix)
    inverse = invert_lower(parent)
    summed = jnp.einsum(
        "nji,njr->nir", even_upper, projected[0::2], precision=precise
    ) + jnp.einsum("nji,njr->nir", odd_upper, projected[1::2], precision=precise)
    return (
        upper_blocks,
        parent,
        inverse,
        jnp.einsum("nik,nkr->nir", inverse, summed, precision=precise),
    )


def pick_block(stacked, position):
    return lax.dynamic_index_in_dim(stacked, position, 0, keepdims=False)


def climb_pairs(factor, projected, transfers, couplings, position, node_count, swap_step):
    records = []
    offset = 0
    level_nodes = node_count
    for level_bit in range(node_count.bit_length() - 1):
        payload = jnp.concatenate([factor, projected], axis=1)
        received = swap_step(payload, level_bit)
        other_factor = received[:, :RANK]
        other_vector = received[:, RANK:]
        node_index = position >> level_bit
        is_even = node_index & 1 == 0
        own_transfer = pick_block(transfers, offset + node_index)
        other_transfer = pick_block(transfers, offset + (node_index ^ 1))
        own_upper = jnp.dot(factor.T, own_transfer, precision=precise)
        other_upper = jnp.dot(other_factor.T, other_transfer, precision=precise)
        even_upper = jnp.where(is_even, own_upper, other_upper)
        odd_upper = jnp.where(is_even, other_upper, own_upper)
        even_vector = jnp.where(is_even, projected, other_vector)
        odd_vector = jnp.where(is_even, other_vector, projected)
        gram_matrix = jnp.dot(even_upper.T, even_upper, precision=precise) + jnp.dot(
            odd_upper.T, odd_upper, precision=precise
        )
        parent = jnp.linalg.cholesky(gram_matrix)
        inverse = invert_lower(parent)
        summed = jnp.dot(even_upper.T, even_vector, precision=precise) + jnp.dot(
            odd_upper.T, odd_vector, precision=precise
        )
        records.append(
            (own_upper, inverse, other_vector, pick_block(couplings, offset + node_index))
        )
        factor = parent
        projected = jnp.dot(inverse, summed, precision=precise)
        offset += level_nodes
        level_nodes //= 2
    return (factor, projected, records)


def shards(
    rhs,
    leaf_basis,
    near_blocks,
    near_partner,
    local_transfer,
    local_coupling,
    far_partner,
    dev_transfer,
    dev_coupling,
    grp_transfer,
    grp_coupling,
):
    dev_count = lax.axis_size("dev")
    grp_count = lax.axis_size("grp")
    dev_place = lax.axis_index("dev")
    grp_place = lax.axis_index("grp")
    device_place = grp_place * dev_count + dev_place
    point_span = LEAF_DEV * LEAF
    node_span = LOCAL_NODES * RANK
    leaf_bases = leaf_basis.reshape(LEAF, LEAF_DEV, RANK).transpose(1, 0, 2)
    points = rhs.reshape(NRHS, LEAF_DEV, LEAF)
    factors = jnp.linalg.cholesky(
        jnp.einsum("lpi,lpk->lik", leaf_bases, leaf_bases, precision=precise)
    )
    leaf_inverse = invert_lower(factors)
    projected = jnp.einsum(
        "lik,lkr->lir",
        leaf_inverse,
        jnp.einsum("lpk,rlp->lkr", leaf_bases, points, precision=precise),
        precision=precise,
    )
    local_trans = blocks_of(local_transfer, LOCAL_NODES)
    local_couple = blocks_of(local_coupling, LOCAL_NODES)
    level_inverses = [leaf_inverse]
    level_upper = []
    level_vectors = []
    offset = 0
    for tree_level in range(LOC):
        level_nodes = LEAF_DEV >> tree_level
        level_vectors.append(projected)
        upper_blocks, factors, inverses, projected = combine(
            factors, projected, local_trans[offset : offset + level_nodes]
        )
        level_upper.append(upper_blocks)
        level_inverses.append(inverses)
        offset += level_nodes
    node_values = jnp.concatenate(level_vectors, axis=0)
    node_flat = node_values.transpose(2, 0, 1).reshape(NRHS, node_span)
    packed = jnp.concatenate([rhs, node_flat], axis=1)
    full_span = point_span + node_span
    padded = with_halo(packed, ((("grp", "dev"), 1),), full_span)
    lower_rim = padded[:, :full_span]
    upper_rim = padded[:, 2 * full_span :]
    point_lower = lower_rim[:, :point_span]
    point_upper = upper_rim[:, :point_span]
    node_lower = lower_rim[:, point_span:]
    node_upper = upper_rim[:, point_span:]
    point_extended = jnp.concatenate([point_lower, rhs, point_upper], axis=1).reshape(
        NRHS, 3 * LEAF_DEV, LEAF
    )
    near_index = near_partner - (device_place - 1) * LEAF_DEV
    partner_points = jnp.take(point_extended, near_index, axis=1)
    near_grid = near_blocks.reshape(LEAF, LEAF_DEV, 2, LEAF)
    near_part = jnp.einsum(
        "plq,rlq->rlp", near_grid[:, :, 0], points, precision=precise
    ) + jnp.einsum("plq,rlq->rlp", near_grid[:, :, 1], partner_points, precision=precise)
    lower_nodes = node_lower.reshape(NRHS, LOCAL_NODES, RANK)
    own_nodes = node_flat.reshape(NRHS, LOCAL_NODES, RANK)
    upper_nodes = node_upper.reshape(NRHS, LOCAL_NODES, RANK)
    coupled_levels = []
    offset = 0
    for tree_level in range(LOC):
        level_nodes = LEAF_DEV >> tree_level
        window = jnp.concatenate(
            [
                lower_nodes[:, offset : offset + level_nodes],
                own_nodes[:, offset : offset + level_nodes],
                upper_nodes[:, offset : offset + level_nodes],
            ],
            axis=1,
        )
        partner_slot = (
            far_partner[0, offset : offset + level_nodes] - (device_place - 1) * level_nodes
        )
        partner_nodes = jnp.take(window, partner_slot, axis=1)
        coupled_levels.append(
            jnp.einsum(
                "nik,rnk->nir",
                local_couple[offset : offset + level_nodes],
                partner_nodes,
                precision=precise,
            )
        )
        offset += level_nodes
    dev_trans = blocks_of(dev_transfer[0], dev_transfer.shape[2] // RANK)
    dev_couple = blocks_of(dev_coupling[0], dev_coupling.shape[2] // RANK)
    grp_trans = blocks_of(grp_transfer, grp_transfer.shape[1] // RANK)
    grp_couple = blocks_of(grp_coupling, grp_coupling.shape[1] // RANK)
    group_factor, group_vector, dev_records = climb_pairs(
        factors[0],
        projected[0],
        dev_trans,
        dev_couple,
        dev_place,
        dev_count,
        lambda payload, bit_index: partner(payload, "dev", bit_index),
    )
    root_factor, root_vector, grp_records = climb_pairs(
        group_factor,
        group_vector,
        grp_trans,
        grp_couple,
        grp_place,
        grp_count,
        lambda payload, bit_index: partner(payload, "grp", bit_index),
    )
    downward = jnp.zeros((RANK, NRHS), jnp.float32)
    for own_upper, inverse, other_vector, coupling in reversed(dev_records + grp_records):
        lifted = jnp.dot(inverse.T, downward, precision=precise)
        downward = jnp.dot(coupling, other_vector, precision=precise) + jnp.dot(
            own_upper, lifted, precision=precise
        )
    downward = downward[None]
    for tree_level in reversed(range(LOC)):
        lifted = jnp.einsum(
            "nki,nkr->nir", level_inverses[tree_level + 1], downward, precision=precise
        )
        downward = coupled_levels[tree_level] + jnp.einsum(
            "nik,nkr->nir",
            level_upper[tree_level],
            jnp.repeat(lifted, 2, axis=0),
            precision=precise,
        )
    lifted = jnp.einsum("nki,nkr->nir", level_inverses[0], downward, precision=precise)
    far_part = jnp.einsum("lpk,lkr->rlp", leaf_bases, lifted, precision=precise)
    product = (near_part + far_part).reshape(NRHS, point_span)
    return (product, root_factor)


def solution(mesh):
    return jax.shard_map(
        shards,
        mesh=mesh,
        in_specs=(
            P(None, ("grp", "dev")),
            P(None, ("grp", "dev")),
            P(None, ("grp", "dev")),
            P(("grp", "dev")),
            P(None, ("grp", "dev")),
            P(None, ("grp", "dev")),
            P(("grp", "dev"), None),
            P("grp", None, None),
            P("grp", None, None),
            P(),
            P(),
        ),
        out_specs=(P(None, ("grp", "dev")), P()),
        check_vma=False,
    )
```

profile of v0, /device:TPU:6, one launch (start us, length us, event | category | flops | bytes accessed | tf_op | source)
XLA Modules:
  0.0 670.1 jit_solution(16051151451745660884)
XLA Ops:
  3.3 93.8 %custom-call.41 = f32[16,64,64]{2,1,0:T(8,128)S(1)} custom-call(f32[16,64,64]{2,1,0:T(8,128)S(1)} %fusion.8), custom_call_target="Cholesky" | custom-call | tf_op jit(solution)/shard_map/jit(cholesky)/cholesky | solution.py:130
  102.0 46.9 %custom-call.43 = f32[8,64,64]{2,1,0:T(8,128)S(1)} custom-call(f32[8,64,64]{2,1,0:T(8,128)S(1)} %fusion.23), custom_call_target="Cholesky" | custom-call | tf_op jit(solution)/shard_map/jit(cholesky)/cholesky | solution.py:54
  151.7 23.5 %custom-call.45 = f32[4,64,64]{2,1,0:T(8,128)S(1)} custom-call(f32[4,64,64]{2,1,0:T(8,128)S(1)} %fusion.42), custom_call_target="Cholesky" | custom-call | tf_op jit(solution)/shard_map/jit(cholesky)/cholesky | solution.py:54
  178.2 39.3 %custom-call.44 = f32[8,1,64,64]{2,3,1,0:T(8,128)S(1)} custom-call(f32[8,1,64,64]{3,2,1,0:T(8,128)S(1)} %select_bitcast_fusion.1), custom_call_target="InvertDiagBlocksLowerTriangular" | custom-call | tf_op jit(solution)/shard_map/jit(_solve_triangular)/vmap()/triangular_solve | solution.py:44
  217.5 78.9 %custom-call.42 = f32[16,1,64,64]{2,3,1,0:T(8,128)S(1)} custom-call(f32[16,1,64,64]{3,2,1,0:T(8,128)S(1)} %select_bitcast_fusion), custom_call_target="InvertDiagBlocksLowerTriangular" | custom-call | tf_op jit(solution)/shard_map/jit(_solve_triangular)/vmap()/triangular_solve | solution.py:44
  301.3 20.4 %custom-call.46 = f32[4,1,64,64]{2,3,1,0:T(8,128)S(1)} custom-call(f32[4,1,64,64]{3,2,1,0:T(8,128)} %select_bitcast_fusion.2), custom_call_target="InvertDiagBlocksLowerTriangular" | custom-call | tf_op jit(solution)/shard_map/jit(_solve_triangular)/vmap()/triangular_solve | solution.py:44
  323.5 11.7 %custom-call.47 = f32[2,64,64]{2,1,0:T(8,128)S(1)} custom-call(f32[2,64,64]{2,1,0:T(8,128)S(1)} %fusion.84), custom_call_target="Cholesky" | custom-call | tf_op jit(solution)/shard_map/jit(cholesky)/cholesky | solution.py:54
  335.4 9.8 %custom-call.48 = f32[2,1,64,64]{2,3,1,0:T(8,128)S(1)} custom-call(f32[2,1,64,64]{3,2,1,0:T(8,128)S(1)} %select_bitcast_fusion.3), custom_call_target="InvertDiagBlocksLowerTriangular" | custom-call | tf_op jit(solution)/shard_map/jit(_solve_triangular)/vmap()/triangular_solve | solution.py:44
  350.7 13.6 %collective-permute-start.1 = (f32[16,2944]{1,0:T(8,128)}, f32[16,2944]{1,0:T(8,128)}, u32[]{:S(2)}, u32[]{:S(2)}) collective-permute-start(f32[16,2944]{1,0:T(8,128)} %constant_dynamic-update-slice_fusion), channel_id=1, source_target_pairs={{1,0},{2,1},{3,2},{4,3},{5,4},{6,5},{7,6},{8,7},{9,8},{10,9},{11,1... | collective-permute-start | bytes 565256 | tf_op jit(solution)/shard_map/ppermute | solution.py:27
  367.6 6.6 custom-call.49
  376.2 5.7 custom-call.59
  424.7 5.8 cholesky.351
  431.8 4.9 custom-call.60
  446.0 5.8 cholesky.362
  466.8 5.8 cholesky.373
  482.2 7.9 %collective-permute-done.5 = f32[64,80]{1,0:T(8,128)S(1)} collective-permute-done((f32[64,80]{1,0:T(8,128)S(1)}, f32[64,80]{1,0:T(8,128)S(1)}, u32[]{:S(2)}, u32[]{:S(2)}) %collective-permute-start.5) | collective-permute-done | bytes 20512 | tf_op jit(solution)/shard_map/ppermute | solution.py:35
  491.0 5.8 cholesky.384
  504.1 7.3 %collective-permute-start.6 = (f32[64,80]{1,0:T(8,128)S(1)}, f32[64,80]{1,0:T(8,128)S(1)}, u32[]{:S(2)}, u32[]{:S(2)}) collective-permute-start(f32[64,80]{1,0:T(8,128)S(1)} %pad_maximum_fusion.9), channel_id=1, source_target_pairs={{0,16},{1,17},{2,18},{3,19},{4,20},{5,21},{6,22},{7,23},{8,24},{9,... | collective-permute-start | bytes 61448 | tf_op jit(solution)/shard_map/ppermute | solution.py:35
  511.6 7.0 %collective-permute-done.6 = f32[64,80]{1,0:T(8,128)S(1)} collective-permute-done((f32[64,80]{1,0:T(8,128)S(1)}, f32[64,80]{1,0:T(8,128)S(1)}, u32[]{:S(2)}, u32[]{:S(2)}) %collective-permute-start.6) | collective-permute-done | bytes 20512 | tf_op jit(solution)/shard_map/ppermute | solution.py:35
  519.4 5.8 cholesky.395
  539.3 5.8 cholesky.406
  560.6 5.8 cholesky.417
  580.4 5.8 cholesky.428
  601.8 5.8 cholesky.439
  (440 shorter events, 237.4 us)
Async XLA Ops:
  101.9 75.5 %copy-start.10 = (f32[16,1024]{1,0:T(8,128)S(1)}, f32[16,1024]{1,0:T(8,128)}, u32[]{:S(2)}) copy-start(f32[16,1024]{1,0:T(8,128)} %param.16) | copy-start | bytes 196612
  177.5 122.8 %copy-start.5 = (f32[16,16,64]{2,1,0:T(8,128)}, f32[16,16,64]{2,1,0:T(8,128)S(1)}, u32[]{:S(2)}) copy-start(f32[16,16,64]{2,1,0:T(8,128)S(1)} %reshape.326) | copy-start | bytes 196612
  346.2 73.8 %copy-start.2 = (f32[16,30,64]{2,0,1:T(8,128)}, f32[16,30,64]{2,0,1:T(8,128)S(1)}, u32[]{:S(2)}) copy-start(f32[16,30,64]{2,0,1:T(8,128)S(1)} %maximum_bitcast_fusion) | copy-start | bytes 368644
  348.8 284.6 %collective-permute-start = (f32[16,2944]{1,0:T(8,128)}, f32[16,2944]{1,0:T(8,128)}, u32[]{:S(2)}, u32[]{:S(2)}) collective-permute-start(f32[16,2944]{1,0:T(8,128)} %constant_dynamic-update-slice_fusion), channel_id=1, source_target_pairs={{0,1},{1,2},{2,3},{3,4},{4,5},{5,6},{6,7},{7,8},{8,9},{9,10},{10,1... | collective-permute-start | bytes 565256 | tf_op jit(solution)/shard_map/ppermute | solution.py:25
  350.7 286.7 %collective-permute-start.1 = (f32[16,2944]{1,0:T(8,128)}, f32[16,2944]{1,0:T(8,128)}, u32[]{:S(2)}, u32[]{:S(2)}) collective-permute-start(f32[16,2944]{1,0:T(8,128)} %constant_dynamic-update-slice_fusion), channel_id=1, source_target_pairs={{1,0},{2,1},{3,2},{4,3},{5,4},{6,5},{7,6},{8,7},{9,8},{10,9},{11,1... | collective-permute-start | bytes 565256 | tf_op jit(solution)/shard_map/ppermute | solution.py:27
  384.3 38.8 %collective-permute-start.2 = (f32[64,80]{1,0:T(8,128)}, f32[64,80]{1,0:T(8,128)}, u32[]{:S(2)}, u32[]{:S(2)}) collective-permute-start(f32[64,80]{1,0:T(8,128)} %pad_maximum_fusion.5), channel_id=1, source_target_pairs={{0,1},{1,0},{2,3},{3,2},{4,5},{5,4},{6,7},{7,6},{8,9},{9,8},{10,11... | collective-permute-start | bytes 61448 | tf_op jit(solution)/shard_map/ppermute | solution.py:35
  438.0 73.3 %copy-start.41 = (f32[64,1,64]{2,1,0:T(1,128)S(1)}, f32[64,1,64]{2,1,0:T(1,128)}, u32[]{:S(2)}) copy-start(f32[64,1,64]{2,1,0:T(1,128)} %get-tuple-element.35) | copy-start | bytes 49156
  438.0 80.5 %copy-start.39 = (f32[64,1,64]{2,1,0:T(1,128)S(1)}, f32[64,1,64]{2,1,0:T(1,128)}, u32[]{:S(2)}) copy-start(f32[64,1,64]{2,1,0:T(1,128)} %get-tuple-element.34) | copy-start | bytes 49156
  439.4 5.8 collective-permute-start.3
  458.7 75.9 %copy-start.44 = (f32[64,1,64]{2,1,0:T(1,128)S(1)}, f32[64,1,64]{2,1,0:T(1,128)}, u32[]{:S(2)}) copy-start(f32[64,1,64]{2,1,0:T(1,128)} %get-tuple-element.55) | copy-start | bytes 49156
  458.7 79.8 %copy-start.42 = (f32[64,1,64]{2,1,0:T(1,128)S(1)}, f32[64,1,64]{2,1,0:T(1,128)}, u32[]{:S(2)}) copy-start(f32[64,1,64]{2,1,0:T(1,128)} %get-tuple-element.54) | copy-start | bytes 49156
  459.2 6.7 collective-permute-start.4
  479.4 75.9 %copy-start.40 = (f32[64,1,64]{2,1,0:T(1,128)S(1)}, f32[64,1,64]{2,1,0:T(1,128)}, u32[]{:S(2)}) copy-start(f32[64,1,64]{2,1,0:T(1,128)} %get-tuple-element.53) | copy-start | bytes 49156
  479.4 80.3 %copy-start.38 = (f32[64,1,64]{2,1,0:T(1,128)S(1)}, f32[64,1,64]{2,1,0:T(1,128)}, u32[]{:S(2)}) copy-start(f32[64,1,64]{2,1,0:T(1,128)} %get-tuple-element.52) | copy-start | bytes 49156
  480.0 10.1 %collective-permute-start.5 = (f32[64,80]{1,0:T(8,128)S(1)}, f32[64,80]{1,0:T(8,128)S(1)}, u32[]{:S(2)}, u32[]{:S(2)}) collective-permute-start(f32[64,80]{1,0:T(8,128)S(1)} %pad_maximum_fusion.8), channel_id=1, source_target_pairs={{0,8},{1,9},{2,10},{3,11},{4,12},{5,13},{6,14},{7,15},{8,0},{9,1},... | collective-permute-start | bytes 61448 | tf_op jit(solution)/shard_map/ppermute | solution.py:35
  503.5 72.7 %copy-start.37 = (f32[64,1,64]{2,1,0:T(1,128)S(1)}, f32[64,1,64]{2,1,0:T(1,128)}, u32[]{:S(2)}) copy-start(f32[64,1,64]{2,1,0:T(1,128)} %get-tuple-element.51) | copy-start | bytes 49156
  503.5 76.1 %copy-start.36 = (f32[64,1,64]{2,1,0:T(1,128)S(1)}, f32[64,1,64]{2,1,0:T(1,128)}, u32[]{:S(2)}) copy-start(f32[64,1,64]{2,1,0:T(1,128)} %get-tuple-element.50) | copy-start | bytes 49156
  504.1 14.5 %collective-permute-start.6 = (f32[64,80]{1,0:T(8,128)S(1)}, f32[64,80]{1,0:T(8,128)S(1)}, u32[]{:S(2)}, u32[]{:S(2)}) collective-permute-start(f32[64,80]{1,0:T(8,128)S(1)} %pad_maximum_fusion.9), channel_id=1, source_target_pairs={{0,16},{1,17},{2,18},{3,19},{4,20},{5,21},{6,22},{7,23},{8,24},{9,... | collective-permute-start | bytes 61448 | tf_op jit(solution)/shard_map/ppermute | solution.py:35
  532.1 68.9 %copy-start.34 = (f32[64,1,64]{2,1,0:T(1,128)S(1)}, f32[64,1,64]{2,1,0:T(1,128)}, u32[]{:S(2)}) copy-start(f32[64,1,64]{2,1,0:T(1,128)} %get-tuple-element.48) | copy-start | bytes 49156
  532.6 5.8 collective-permute-start.7
  539.2 75.7 %copy-start.50 = (f32[64,1,64]{2,1,0:T(1,128)S(1)}, f32[64,1,64]{2,1,0:T(1,128)}, u32[]{:S(2)}) copy-start(f32[64,1,64]{2,1,0:T(1,128)} %get-tuple-element.69) | copy-start | bytes 49156
  552.5 7.3 %collective-permute-start.8 = (f32[64,80]{1,0:T(8,128)S(1)}, f32[64,80]{1,0:T(8,128)S(1)}, u32[]{:S(2)}, u32[]{:S(2)}) collective-permute-start(f32[64,80]{1,0:T(8,128)S(1)} %pad_maximum_fusion.11), channel_id=1, source_target_pairs={{0,64},{32,96},{64,0},{96,32},{128,192},{160,224},{192,128},{224,1... | collective-permute-start | bytes 61448 | tf_op jit(solution)/shard_map/ppermute | solution.py:35
  573.8 5.8 collective-permute-start.9
  593.6 7.3 %collective-permute-start.10 = (f32[64,80]{1,0:T(8,128)S(1)}, f32[64,80]{1,0:T(8,128)S(1)}, u32[]{:S(2)}, u32[]{:S(2)}) collective-permute-start(f32[64,80]{1,0:T(8,128)S(1)} %pad_maximum_fusion.13), channel_id=1, source_target_pairs={{0,256},{32,288},{64,320},{96,352},{128,384},{160,416},{192,448},{... | collective-permute-start | bytes 61448 | tf_op jit(solution)/shard_map/ppermute | solution.py:35
  (47 other events, 1027.5 us)
where the time goes:
time: 682 us; the launch traced here: 670 us
  other arithmetic  466 us (68%)
  matrix products  70.3 us (10%)
  local copies, waits for them, and re-layouts  52.3 us (8%)
  starting transfers between devices  40.6 us (6%)
  waiting for transfers between devices  38 us (6%)
    another operation x29, other arithmetic, invert_lower(): return jax.scipy.linalg.solve_triangular(factor, identity, lower=True)  207 us
    another operation x4, other arithmetic, shards(): jnp.linalg.cholesky(jnp.einsum('lpi,lpk->lik', leaf_bases, leaf_bases, pr...  94 us
    another operation x12, other arithmetic, combine(): parent = jnp.linalg.cholesky(gram_matrix)  89.8 us
    another operation x27, other arithmetic, climb_pairs(): parent = jnp.linalg.cholesky(gram_matrix)  58.7 us
    ppermute x9, waiting for transfers between devices, partner(): lax.ppermute(array, axis, [(i, i ^ 1 << bit) for i in range(lax.axis_size...  38 us
    ppermute x9, starting transfers between devices, partner(): lax.ppermute(array, axis, [(i, i ^ 1 << bit) for i in range(lax.axis_size...  25.1 us
  transfers between devices with their start and end apart: 11, of which 8 were waited for; matrix products, arithmetic and copies ran while one was open for 31% of the time, Pallas kernels for 0%

commit v1 on v0

v1 whole, which is shorter than its diff:
```python
import jax
import jax.numpy as jnp
from jax import lax
from jax.experimental import pallas as pl
from jax.experimental.pallas import tpu as pltpu
from jax.sharding import PartitionSpec as P

RANK = 64
NRHS = 16
LOC_PAIRS = 15
PAIR_BASE = (0, 8, 12, 14)
LOG_DEV = 5
LOG_GRP = 4
UP = LOG_DEV + LOG_GRP
BLOCK = 16
CHUNK = 5
MESH = pl.DeviceIdType.MESH
f32 = jnp.float32


def dot(a, b, ca, cb):
    return lax.dot_general(
        a,
        b,
        (((ca,), (cb,)), ((), ())),
        precision=lax.Precision.HIGHEST,
        preferred_element_type=f32,
    )


def nn(a, b):
    return dot(a, b, 1, 0)


def nt(a, b):
    return dot(a, b, 1, 1)


def tn(a, b):
    return dot(a, b, 0, 0)


def left_of(rows):
    return lax.broadcasted_iota(jnp.int32, (rows, 128), 1) < 64


def swap(p):
    return pltpu.roll(p, 64, 1)


def fold(p):
    return p + swap(p)


def pick(a, b):
    return jnp.where(left_of(a.shape[0]), a, b)


def bd(p):
    left = left_of(64)
    return jnp.concatenate([jnp.where(left, p, 0.0), jnp.where(left, 0.0, p)], axis=0)


def diag(c):
    return pick(c[:64], c[64:])


def dups(p):
    s = swap(p)
    return pick(p, s), pick(s, p)


def merge(g, z, e):
    be = bd(e)
    return fold(diag(tn(be, nn(bd(g), be)))), fold(nn(z, be))


def factor_chunk(load, store, scratch, pairs):
    row = lax.broadcasted_iota(jnp.int32, (64, 128), 0)
    lane = lax.broadcasted_iota(jnp.int32, (64, 128), 1)
    left = lane < 64
    eye_left = jnp.where(row == lane, 1.0, 0.0)
    eye_right = jnp.where(row == lane - 64, 1.0, 0.0)
    for p in range(pairs):
        s = swap(load(p))
        scratch[2 * p] = jnp.where(left, eye_left, s)
        scratch[2 * p + 1] = jnp.where(left, s, eye_right)
    nodes = 2 * pairs
    rows = lax.broadcasted_iota(jnp.int32, (BLOCK, 128), 0)
    for k in range(64 // BLOCK):
        lo = k * BLOCK
        cur = [scratch[n, lo : lo + BLOCK, :] for n in range(nodes)]
        piv = [jnp.ones((BLOCK, 128), f32)] * nodes
        for j in range(BLOCK):
            below = rows > j
            here = rows == j
            for n in range(nodes):
                c = lo + j + (64 if n % 2 == 0 else 0)
                r = cur[n]
                col = jnp.broadcast_to(r[:, c : c + 1], (BLOCK, 128))
                d = jnp.broadcast_to(col[j : j + 1, :], (BLOCK, 128))
                top = jnp.broadcast_to(r[j : j + 1, :], (BLOCK, 128))
                piv[n] = jnp.where(here, d, piv[n])
                if j < BLOCK - 1:
                    cur[n] = r - jnp.where(below, col, 0.0) * (top / d)
        for n in range(nodes):
            done = cur[n] * lax.rsqrt(piv[n])
            scratch[n, lo : lo + BLOCK, :] = done
            if lo + BLOCK < 64:
                half = 64 if n % 2 == 0 else 0
                left_rows = done.T[half + lo + BLOCK : half + 64, :]
                scratch[n, lo + BLOCK : 64, :] -= nn(left_rows, done)
    for p in range(pairs):
        store(p, jnp.where(left, scratch[2 * p], scratch[2 * p + 1]))


def factor_all(grams, inverses, scratch, count):
    @pl.loop(0, count // CHUNK)
    def _(i):
        def load(p):
            return grams[i * CHUNK + p]

        def store(p, value):
            inverses[i * CHUNK + p] = value

        factor_chunk(load, store, scratch, CHUNK)


def lanes(i):
    return slice(128 * i, 128 * i + 128)


def up_local(leaf, rhs, trans, grams, zs):
    for j in range(8):
        u = leaf[:, lanes(j)]
        grams[j] = diag(tn(u, u))
        zs[j] = nn(rhs[:, lanes(j)], bd(u))
    for k in range(4):
        base = PAIR_BASE[k]
        held = None
        for i in range(8 >> k):
            g, z = merge(grams[base + i], zs[base + i], trans[:, lanes(base + i)])
            if k == 3:
                return g, z
            if i % 2 == 0:
                held = (g, z)
            else:
                grams[PAIR_BASE[k + 1] + i // 2] = pick(held[0], g)
                zs[PAIR_BASE[k + 1] + i // 2] = pick(held[1], z)


def pack(g, z):
    return pick(g[:32], g[32:]), pick(z[:8], z[8:])


def unpack(pg, pz):
    g0, g1 = dups(pg)
    z0, z1 = dups(pz)
    return jnp.concatenate([g0, g1], 0), jnp.concatenate([z0, z1], 0)


def kernel_a(leaf, rhs, trans, inv, xhat, top, grams, zs, scratch):
    g, z = up_local(leaf, rhs, trans, grams, zs)
    pg, pz = pack(g, z)
    top[0:32, :] = pg
    top[32:40, :] = pz
    factor_all(grams, inv, scratch, LOC_PAIRS)
    for i in range(LOC_PAIRS):
        xhat[i] = nt(zs[i], bd(inv[i]))


def kernel_b(
    rhs,
    xhat,
    top,
    dev_trans,
    grp_trans,
    up_g,
    up_z,
    root_g,
    rhs_lo,
    rhs_hi,
    xhat_lo,
    xhat_hi,
    outgoing,
    incoming,
    send_sem,
    recv_sem,
    halo_send,
    halo_recv,
):
    grp = lax.axis_index("grp")
    dev = lax.axis_index("dev")
    place = grp * 32 + dev
    after = lax.rem(place + 1, 512)
    before = lax.rem(place + 511, 512)
    right = (after // 32, lax.rem(after, 32))
    left = (before // 32, lax.rem(before, 32))
    peers = []
    for b in range(UP):
        if b < LOG_DEV:
            bit = lax.rem(dev // (1 << b), 2)
            peers.append((grp, dev + (1 - 2 * bit) * (1 << b)))
        else:
            w = 1 << (b - LOG_DEV)
            bit = lax.rem(grp // w, 2)
            peers.append((grp + (1 - 2 * bit) * w, dev))
    barrier = pltpu.get_barrier_semaphore()
    for peer in peers + [left, right]:
        pl.semaphore_signal(barrier, inc=1, device_id=peer, device_id_type=MESH)
    pl.semaphore_wait(barrier, UP + 2)

    def copy(src, dst, s, r, peer):
        return pltpu.make_async_remote_copy(
            src_ref=src,
            dst_ref=dst,
            send_sem=s,
            recv_sem=r,
            device_id=peer,
            device_id_type=MESH,
        )

    halos = [
        copy(rhs, rhs_lo, halo_send.at[0], halo_recv.at[0], right),
        copy(rhs, rhs_hi, halo_send.at[1], halo_recv.at[1], left),
        copy(xhat, xhat_lo, halo_send.at[2], halo_recv.at[2], right),
        copy(xhat, xhat_hi, halo_send.at[3], halo_recv.at[3], left),
    ]
    outgoing[0] = top[...]
    own_g, own_z = unpack(top[0:32, :], top[32:40, :])
    half = lax.broadcasted_iota(jnp.int32, (64, 128), 1) // 64
    for b in range(UP):
        step = copy(
            outgoing.at[b], incoming.at[b], send_sem.at[b], recv_sem.at[b], peers[b]
        )
        step.start()
        if b < 4:
            halos[b].start()
        pos = dev if b < LOG_DEV else grp
        lev = b if b < LOG_DEV else b - LOG_DEV
        size = 32 if b < LOG_DEV else 16
        bit = lax.rem(pos // (1 << lev), 2)
        pair = size - (size >> lev) + pos // (2 << lev)
        at = pl.ds(pl.multiple_of(pair * 128, 128), 128)
        e = dev_trans[0, :, at] if b < LOG_DEV else grp_trans[:, at]
        mine = half == bit
        step.wait()
        sib_g, sib_z = unpack(incoming[b, 0:32, :], incoming[b, 32:40, :])
        g = jnp.where(mine, own_g, sib_g)
        z = jnp.where(mine[:16], own_z, sib_z)
        up_g[b] = g
        up_z[b] = z
        own_g, own_z = merge(g, z, e)
        if b + 1 < UP:
            pg, pz = pack(own_g, own_z)
            outgoing[b + 1, 0:32, :] = pg
            outgoing[b + 1, 32:40, :] = pz
    root_g[...] = own_g
    for halo in halos:
        halo.wait()


def kernel_c(
    info,
    near_at,
    far_at,
    leaf,
    rhs,
    rhs_lo,
    rhs_hi,
    near,
    trans,
    couple,
    inv,
    xhat,
    xhat_lo,
    xhat_hi,
    up_g,
    up_z,
    root_g,
    dev_trans,
    dev_couple,
    grp_trans,
    grp_couple,
    product,
    root,
    grams,
    up_inv,
    scratch,
    points,
    nodes,
):
    half = lax.broadcasted_iota(jnp.int32, (16, 128), 1) // 64
    for i in range(UP):
        grams[i] = up_g[i]
    grams[UP] = root_g[...]
    factor_all(grams, up_inv, scratch, UP + 1)
    last = scratch[2 * CHUNK - 1]
    upper = lax.broadcasted_iota(jnp.int32, (64, 128), 0) <= lax.broadcasted_iota(
        jnp.int32, (64, 128), 1
    )
    root[...] = jnp.where(upper, last, 0.0)[:, :64].T

    for s, block in enumerate((rhs_lo, rhs, rhs_hi)):
        for j in range(8):
            a, b = dups(block[:, lanes(j)])
            points[16 * s + 2 * j] = a
            points[16 * s + 2 * j + 1] = b
    for k in range(4):
        size = 16 >> k
        for s, block in enumerate((xhat_lo, xhat, xhat_hi)):
            for j in range(size // 2):
                a, b = dups(block[PAIR_BASE[k] + j])
                at = 6 * PAIR_BASE[k] + size * s + 2 * j
                nodes[at] = a
                nodes[at + 1] = b

    v = None
    for b in reversed(range(UP)):
        pos = info[1] if b < LOG_DEV else info[0]
        lev = b if b < LOG_DEV else b - LOG_DEV
        size = 32 if b < LOG_DEV else 16
        bit = lax.rem(pos // (1 << lev), 2)
        pair = size - (size >> lev) + pos // (2 << lev)
        at = pl.ds(pl.multiple_of(pair * 128, 128), 128)
        e = dev_trans[0, :, at] if b < LOG_DEV else grp_trans[:, at]
        c = dev_couple[0, :, at] if b < LOG_DEV else grp_couple[:, at]
        bi = bd(up_inv[b])
        t = nn(nt(swap(nt(up_z[b], bi)), bd(c)), bi)
        if v is not None:
            t = t + nt(v, bd(e))
        v = jnp.where(half == bit, t, swap(t))

    held = [v]
    for k in reversed(range(4)):
        base = PAIR_BASE[k]
        grown = []
        for i in range(8 >> k):
            p = base + i
            qa = 6 * base + far_at[2 * p]
            qb = 6 * base + far_at[2 * p + 1]
            x = pick(nodes[qa], nodes[qb])
            y = nt(x, bd(couple[:, lanes(p)]))
            t = nn(y, bd(inv[p])) + nt(held[i], bd(trans[:, lanes(p)]))
            if k > 0:
                grown.extend(dups(t))
            else:
                far = nt(t, bd(leaf[:, lanes(i)]))
                cat = jnp.concatenate(
                    [
                        pick(points[16 + 2 * i], points[near_at[2 * i]]),
                        pick(points[17 + 2 * i], points[near_at[2 * i + 1]]),
                    ],
                    0,
                )
                d = jnp.concatenate([near[:, lanes(2 * i)], near[:, lanes(2 * i + 1)]], 0)
                o = nt(cat, d)
                product[:, lanes(i)] = pick(o[:16], o[16:]) + far
        held = grown


def shards(
    rhs,
    leaf_basis,
    near_blocks,
    near_partner,
    local_transfer,
    local_coupling,
    far_partner,
    dev_transfer,
    dev_coupling,
    grp_transfer,
    grp_coupling,
):
    dev = lax.axis_index("dev")
    grp = lax.axis_index("grp")
    place = grp * lax.axis_size("dev") + dev
    vmem = pl.BlockSpec(memory_space=pltpu.VMEM)
    smem = pl.BlockSpec(memory_space=pltpu.SMEM)

    def shape(*dims):
        return jax.ShapeDtypeStruct(dims, f32)

    inv, xhat, top = pl.pallas_call(
        kernel_a,
        name="local_up",
        out_shape=(shape(15, 64, 128), shape(15, 16, 128), shape(40, 128)),
        in_specs=[vmem] * 3,
        out_specs=(vmem,) * 3,
        scratch_shapes=[
            pltpu.VMEM((15, 64, 128), f32),
            pltpu.VMEM((15, 16, 128), f32),
            pltpu.VMEM((2 * CHUNK, 64, 128), f32),
        ],
    )(leaf_basis, rhs, local_transfer)

    up_g, up_z, root_g, rhs_lo, rhs_hi, xhat_lo, xhat_hi = pl.pallas_call(
        kernel_b,
        name="climb",
        out_shape=(
            shape(UP, 64, 128),
            shape(UP, 16, 128),
            shape(64, 128),
            shape(16, 1024),
            shape(16, 1024),
            shape(15, 16, 128),
            shape(15, 16, 128),
        ),
        in_specs=[vmem] * 5,
        out_specs=(vmem,) * 7,
        scratch_shapes=[
            pltpu.VMEM((UP, 40, 128), f32),
            pltpu.VMEM((UP, 40, 128), f32),
            pltpu.SemaphoreType.DMA((UP,)),
            pltpu.SemaphoreType.DMA((UP,)),
            pltpu.SemaphoreType.DMA((4,)),
            pltpu.SemaphoreType.DMA((4,)),
        ],
        compiler_params=pltpu.CompilerParams(collective_id=0, has_side_effects=True),
    )(rhs, xhat, top, dev_transfer, grp_transfer)

    sizes = jnp.repeat(jnp.array([16, 8, 4, 2], jnp.int32), jnp.array([16, 8, 4, 2]), total_repeat_length=30)
    info = jnp.stack([grp, dev]).astype(jnp.int32)
    near_at = near_partner - (place - 1) * 16
    far_at = far_partner[0] - (place - 1) * sizes

    return pl.pallas_call(
        kernel_c,
        name="down",
        out_shape=(shape(16, 1024), shape(64, 64)),
        in_specs=[smem] * 3 + [vmem] * 18,
        out_specs=(vmem,) * 2,
        scratch_shapes=[
            pltpu.VMEM((UP + 1, 64, 128), f32),
            pltpu.VMEM((UP + 1, 64, 128), f32),
            pltpu.VMEM((2 * CHUNK, 64, 128), f32),
            pltpu.VMEM((48, 16, 128), f32),
            pltpu.VMEM((90, 16, 128), f32),
        ],
    )(
        info,
        near_at,
        far_at,
        leaf_basis,
        rhs,
        rhs_lo,
        rhs_hi,
        near_blocks,
        local_transfer,
        local_coupling,
        inv,
        xhat,
        xhat_lo,
        xhat_hi,
        up_g,
        up_z,
        root_g,
        dev_transfer,
        dev_coupling,
        grp_transfer,
        grp_coupling,
    )


def solution(mesh):
    return jax.shard_map(
        shards,
        mesh=mesh,
        in_specs=(
            P(None, ("grp", "dev")),
            P(None, ("grp", "dev")),
            P(None, ("grp", "dev")),
            P(("grp", "dev")),
            P(None, ("grp", "dev")),
            P(None, ("grp", "dev")),
            P(("grp", "dev"), None),
            P("grp", None, None),
            P("grp", None, None),
            P(),
            P(),
        ),
        out_specs=(P(None, ("grp", "dev")), P()),
        check_vma=False,
    )
```

time: 682 us -> 131 us (0.19); the launches traced: 670 us -> 130 us
  other arithmetic: 466 us -> 1.7 us
  Pallas kernels: 0 us -> 127 us
  matrix products: 70.3 us -> 0 us
  local copies, waits for them, and re-layouts: 52.3 us -> 0.15 us
  starting transfers between devices: 40.6 us -> 0 us
  waiting for transfers between devices: 38 us -> 0 us
    another operation x72 -> x1, other arithmetic: 449 us -> 0.65 us  [shards(): info = jnp.stack([grp, dev]).astype(jnp.int32)]
    pallas_call x0 -> x3, Pallas kernels: none -> 127 us  [the longest x1 53 us: shards(): pl.pallas_call(kernel_b, name='climb', out_shape=(shape(UP, 64, 128), sha...]
    dot_general x130 -> x0, matrix products: 65.5 us -> none  [the longest x9 8.95 us: shards(): jnp.dot(coupling, other_vector, precision=precise)]
    ppermute x11 -> x0, starting transfers between devices: 40.6 us -> none  [the longest x9 25.1 us: partner(): lax.ppermute(array, axis, [(i, i ^ 1 << bit) for i in range(lax.axis_size...]
    ppermute x11 -> x0, waiting for transfers between devices: 38 us -> none  [the longest x9 38 us: partner(): lax.ppermute(array, axis, [(i, i ^ 1 << bit) for i in range(lax.axis_size...]
    reshape x15 -> x0, local copies, waits for them, and re-layouts: 14.3 us -> none  [the longest x6 8 us: blocks_of(): return matrix.reshape(matrix.shape[0], node_count, -1).transpose(1, 0, 2)]
    slice x22 -> x0, local copies, waits for them, and re-layouts: 12.4 us -> none  [the longest x4 4.11 us: shards(): upper_nodes[:, offset:offset + level_nodes]]
    another operation x4 -> x0, local copies, waits for them, and re-layouts: 12.2 us -> none
  transfers between devices with their start and end apart: 11 -> 0, of which waited for: 8 -> 0; matrix products, arithmetic and copies ran while one was open for 31% -> 0% of each run, Pallas kernels for 0% -> 0%
where the time goes in v1:
time: 131 us; the launch traced here: 130 us
  Pallas kernels  127 us (97%)
  other arithmetic  1.7 us (1%)
    pallas_call x1, Pallas kernels, shards(): pl.pallas_call(kernel_b, name='climb', out_shape=(shape(UP, 64, 128), sha...  53 us
    pallas_call x1, Pallas kernels, shards(): pl.pallas_call(kernel_a, name='local_up', out_shape=(shape(15, 64, 128),...  38 us
    pallas_call x1, Pallas kernels, shards(): pl.pallas_call(kernel_c, name='down', out_shape=(shape(16, 1024), shape(6...  36.4 us

profile of v1, /device:TPU:6, one launch (start us, length us, event | category | flops | bytes accessed | tf_op | source)
XLA Modules:
  0.0 130.0 jit_solution(17472204596918623081)
XLA Ops:
  0.6 0.0 copy-start
  0.6 0.0 copy-start.1
  0.7 0.6 pad_add_fusion.info
  1.3 0.0 copy-done
  1.3 0.0 copy-done.1
  1.3 0.0 copy-start.2
  1.3 0.5 bitcast_subtract_fusion.far_at
  1.8 0.1 copy-done.2
  2.0 0.5 broadcast_subtract_fusion.near_at
  2.5 38.0 %local_up.1 = (f32[15,64,128]{2,1,0:T(8,128)}, f32[15,16,128]{2,1,0:T(8,128)}, f32[40,128]{1,0:T(8,128)}) custom-call(f32[64,1024]{1,0:T(8,128)} %leaf.3, f32[16,1024]{1,0:T(8,128)} %rhs.6, f32[64,1920]{1,0:T(8,128)} %trans.3), custom_call_target="tpu_custom_call" | custom-call | tf_op jit(solution)/shard_map/local_up/pallas_call | solution.py:384
  40.5 53.0 %climb.1 = (f32[9,64,128]{2,1,0:T(8,128)}, f32[9,16,128]{2,1,0:T(8,128)}, f32[64,128]{1,0:T(8,128)}, f32[16,1024]{1,0:T(8,128)}, f32[16,1024]{1,0:T(8,128)}, /*i...) custom-call(f32[16,1024]{1,0:T(8,128)} %rhs.6, f32[15,16,128]{2,1,0:T(8,128)} %get-tuple-element.24.xhat, ...), custom_call_target="tpu_custom_call" | custom-call | tf_op jit(solution)/shard_map/climb/pallas_call | solution.py:397
  93.6 36.4 %down.1 = (f32[16,1024]{1,0:T(8,128)}, f32[64,64]{1,0:T(8,128)}) custom-call(s32[2]{0:T(128)} %pad_add_fusion.info, s32[16]{0:T(128)} %broadcast_subtract_fusion.near_at, s32[30]{0:T(128)} %bitcast_subtract_fusion.far_at, f32[64,1024]{1,0:T(8,128)} %leaf.3, f32[16,1024]{1,0:T(8,128)} %rhs.6, f32[16,1024]{1,0:T(8,128)} %get-tuple-element.26.rhs_lo, ...), custom_call_target="tpu_custom_call" | custom-call | tf_op jit(solution)/shard_map/down/pallas_call | solution.py:427
Async XLA Ops:
  0.6 0.7 copy-start
  0.6 0.7 copy-start.1
  1.3 0.7 copy-start.2

commit v2 on v1

v2 whole, which is shorter than its diff:
```python
import jax
import jax.numpy as jnp
from jax import lax
from jax.experimental import pallas as pl
from jax.experimental.pallas import tpu as pltpu
from jax.sharding import PartitionSpec as P

RANK = 64
NRHS = 16
LOC_PAIRS = 15
PAIR_BASE = (0, 8, 12, 14)
LOG_DEV = 5
LOG_GRP = 4
UP = LOG_DEV + LOG_GRP
FILL = 4
MESH = pl.DeviceIdType.MESH
f32 = jnp.float32
bf16 = jnp.bfloat16


def split(x):
    hi = x.astype(bf16)
    return hi, (x - hi.astype(f32)).astype(bf16)


def mm(a, b, ca, cb):
    return lax.dot_general(
        jnp.concatenate([a[0], a[1], a[0]], axis=ca),
        jnp.concatenate([b[0], b[0], b[1]], axis=cb),
        (((ca,), (cb,)), ((), ())),
        preferred_element_type=f32,
    )


def nn(a, b):
    return mm(a, b, 1, 0)


def nt(a, b):
    return mm(a, b, 1, 1)


def tn(a, b):
    return mm(a, b, 0, 0)


def left_of(rows):
    return lax.broadcasted_iota(jnp.int32, (rows, 128), 1) < 64


def swap(p):
    return pltpu.roll(p, 64, 1)


def fold(p):
    return p + swap(p)


def pick(a, b):
    return jnp.where(left_of(a.shape[0]), a, b)


def bd(pair):
    keep = left_of(64).astype(f32)
    left = keep.astype(bf16)
    right = (1.0 - keep).astype(bf16)
    return tuple(jnp.concatenate([x * left, x * right], axis=0) for x in pair)


def diag(c):
    return pick(c[:64], c[64:])


def dups(p):
    s = swap(p)
    return pick(p, s), pick(s, p)


def merge(g, z, e):
    es = split(e)
    lhs = tuple(jnp.concatenate([a, b], axis=0) for a, b in zip(bd(split(g)), split(z)))
    both = nn(lhs, bd(es))
    return fold(diag(tn(es, split(diag(both[:128]))))), fold(both[128:])


def factor(grams, inverses, scratch, pairs):
    row = lax.broadcasted_iota(jnp.int32, (64, 128), 0)
    lane = lax.broadcasted_iota(jnp.int32, (64, 128), 1)
    left = lane < 64
    eye_left = jnp.where(row == lane, 1.0, 0.0)
    eye_right = jnp.where(row == lane - 64, 1.0, 0.0)
    for p in range(pairs):
        s = swap(grams[p])
        scratch[2 * p] = jnp.where(left, eye_left, s)
        scratch[2 * p + 1] = jnp.where(left, s, eye_right)
    nodes = 2 * pairs
    rows = row[:8]
    for lo in range(0, 64, 16):
        cur = [[scratch[n, lo + h : lo + h + 8, :] for h in (0, 8)] for n in range(nodes)]
        for j in range(16):
            h, js = j // 8, j % 8
            here = rows == js
            below = rows > js
            for n in range(nodes):
                c = lo + j + (64 if n % 2 == 0 else 0)
                r = cur[n][h]
                col = jnp.broadcast_to(r[:, c : c + 1], (8, 128))
                inv = lax.rsqrt(jnp.broadcast_to(col[js : js + 1, :], (8, 128)))
                top = jnp.broadcast_to(r[js : js + 1, :], (8, 128)) * inv
                step = top * inv
                if js < 7:
                    r = r - jnp.where(below, col, 0.0) * step
                cur[n][h] = jnp.where(here, top, r)
                if h == 0:
                    r = cur[n][1]
                    cur[n][1] = r - jnp.broadcast_to(r[:, c : c + 1], (8, 128)) * step
        for n in range(nodes):
            done = jnp.concatenate(cur[n], axis=0)
            scratch[n, lo : lo + 16, :] = done
            if lo + 16 < 64:
                half = 64 if n % 2 == 0 else 0
                hi = done.astype(bf16).astype(f32)
                low = (done - hi).astype(bf16).astype(f32)
                across = jnp.concatenate([hi, low, hi], axis=0).T
                scratch[n, lo + 16 : 64, :] -= lax.dot_general(
                    across[half + lo + 16 : half + 64, :].astype(bf16),
                    jnp.concatenate([hi, hi, low], axis=0).astype(bf16),
                    (((1,), (0,)), ((), ())),
                    preferred_element_type=f32,
                )
    for p in range(pairs):
        inverses[p] = jnp.where(left, scratch[2 * p], scratch[2 * p + 1])


def lanes(i):
    return slice(128 * i, 128 * i + 128)


def up_leaves(leaf, rhs, grams, zs):
    for j in range(8):
        u = split(leaf[:, lanes(j)])
        grams[j] = diag(tn(u, u))
        zs[j] = nn(split(rhs[:, lanes(j)]), bd(u))


def up_local(trans, grams, zs):
    for k in range(4):
        base = PAIR_BASE[k]
        held = None
        for i in range(8 >> k):
            g, z = merge(grams[base + i], zs[base + i], trans[:, lanes(base + i)])
            if k == 3:
                return g, z
            if i % 2 == 0:
                held = (g, z)
            else:
                grams[PAIR_BASE[k + 1] + i // 2] = pick(held[0], g)
                zs[PAIR_BASE[k + 1] + i // 2] = pick(held[1], z)


def pack(g, z):
    return pick(g[:32], g[32:]), pick(z[:8], z[8:])


def unpack(pg, pz):
    g0, g1 = dups(pg)
    z0, z1 = dups(pz)
    return jnp.concatenate([g0, g1], 0), jnp.concatenate([z0, z1], 0)


def level_at(b, grp, dev):
    pos = dev if b < LOG_DEV else grp
    lev = b if b < LOG_DEV else b - LOG_DEV
    size = 32 if b < LOG_DEV else 16
    bit = lax.rem(pos // (1 << lev), 2)
    pair = size - (size >> lev) + pos // (2 << lev)
    return bit, pl.ds(pl.multiple_of(pair * 128, 128), 128)


def upper_block(b, dev_array, grp_array, at):
    return dev_array.at[0, :, at] if b < LOG_DEV else grp_array.at[:, at]


def kernel_climb(
    leaf_hbm,
    rhs_hbm,
    trans_hbm,
    dev_trans,
    grp_trans,
    inv,
    xhat,
    up_g,
    up_z,
    root_g,
    up_e,
    rhs_lo,
    rhs_hi,
    xhat_lo,
    xhat_hi,
    leaf,
    rhs,
    trans,
    grams,
    zs,
    scratch,
    outgoing,
    incoming,
    send_sem,
    recv_sem,
    halo_send,
    halo_recv,
    load_sem,
):
    grp = lax.axis_index("grp")
    dev = lax.axis_index("dev")
    place = grp * 32 + dev
    after = lax.rem(place + 1, 512)
    before = lax.rem(place + 511, 512)
    right = (after // 32, lax.rem(after, 32))
    left = (before // 32, lax.rem(before, 32))
    peers = []
    for b in range(UP):
        w = 1 << (b if b < LOG_DEV else b - LOG_DEV)
        bit, _ = level_at(b, grp, dev)
        if b < LOG_DEV:
            peers.append((grp, dev + (1 - 2 * bit) * w))
        else:
            peers.append((grp + (1 - 2 * bit) * w, dev))
    barrier = pltpu.get_barrier_semaphore()
    for peer in peers + [left, right]:
        pl.semaphore_signal(barrier, inc=1, device_id=peer, device_id_type=MESH)

    loads = [
        pltpu.make_async_copy(src, dst, load_sem.at[i])
        for i, (src, dst) in enumerate(
            [(leaf_hbm, leaf), (rhs_hbm, rhs), (trans_hbm, trans)]
            + [
                (upper_block(b, dev_trans, grp_trans, level_at(b, grp, dev)[1]), up_e.at[b])
                for b in range(UP)
            ]
        )
    ]
    for load in loads:
        load.start()

    def copy(src, dst, s, r, peer):
        return pltpu.make_async_remote_copy(
            src_ref=src,
            dst_ref=dst,
            send_sem=s,
            recv_sem=r,
            device_id=peer,
            device_id_type=MESH,
        )

    halos = [
        copy(rhs, rhs_lo, halo_send.at[0], halo_recv.at[0], right),
        copy(rhs, rhs_hi, halo_send.at[1], halo_recv.at[1], left),
        copy(xhat, xhat_lo, halo_send.at[2], halo_recv.at[2], right),
        copy(xhat, xhat_hi, halo_send.at[3], halo_recv.at[3], left),
    ]
    loads[0].wait()
    loads[1].wait()
    up_leaves(leaf, rhs, grams, zs)
    loads[2].wait()
    own_g, own_z = up_local(trans, grams, zs)
    pg, pz = pack(own_g, own_z)
    outgoing[0, 0:32, :] = pg
    outgoing[0, 32:40, :] = pz
    pl.semaphore_wait(barrier, UP + 2)
    half = lax.broadcasted_iota(jnp.int32, (64, 128), 1) // 64
    for b in range(UP):
        step = copy(
            outgoing.at[b], incoming.at[b], send_sem.at[b], recv_sem.at[b], peers[b]
        )
        step.start()
        if b == 0:
            halos[0].start()
            halos[1].start()
        if b == FILL:
            factor(grams, inv, scratch, LOC_PAIRS)
            for i in range(LOC_PAIRS):
                xhat[i] = nt(split(zs[i]), bd(split(inv[i])))
            halos[2].start()
            halos[3].start()
        mine = half == level_at(b, grp, dev)[0]
        loads[3 + b].wait()
        step.wait()
        sib_g, sib_z = unpack(incoming[b, 0:32, :], incoming[b, 32:40, :])
        g = jnp.where(mine, own_g, sib_g)
        z = jnp.where(mine[:16], own_z, sib_z)
        up_g[b] = g
        up_z[b] = z
        own_g, own_z = merge(g, z, up_e[b])
        if b + 1 < UP:
            pg, pz = pack(own_g, own_z)
            outgoing[b + 1, 0:32, :] = pg
            outgoing[b + 1, 32:40, :] = pz
    root_g[...] = own_g
    for halo in halos:
        halo.wait()


def kernel_down(
    near_partner,
    far_partner,
    up_g,
    up_z,
    root_g,
    up_e,
    dev_couple,
    grp_couple,
    leaf_hbm,
    rhs_hbm,
    rhs_lo_hbm,
    rhs_hi_hbm,
    near_hbm,
    trans_hbm,
    couple_hbm,
    inv_hbm,
    xhat_hbm,
    xhat_lo_hbm,
    xhat_hi_hbm,
    product,
    root,
    leaf,
    rhs,
    rhs_lo,
    rhs_hi,
    near,
    trans,
    couple,
    inv,
    xhat,
    xhat_lo,
    xhat_hi,
    up_s,
    grams,
    up_inv,
    scratch,
    points,
    nodes,
    load_sem,
):
    grp = lax.axis_index("grp")
    dev = lax.axis_index("dev")
    first = grp * 32 + dev - 1
    loads = [
        pltpu.make_async_copy(src, dst, load_sem.at[i])
        for i, (src, dst) in enumerate(
            [
                (upper_block(b, dev_couple, grp_couple, level_at(b, grp, dev)[1]), up_s.at[b])
                for b in range(UP)
            ]
            + [
                (rhs_hbm, rhs),
                (rhs_lo_hbm, rhs_lo),
                (rhs_hi_hbm, rhs_hi),
                (xhat_hbm, xhat),
                (xhat_lo_hbm, xhat_lo),
                (xhat_hi_hbm, xhat_hi),
                (couple_hbm, couple),
                (inv_hbm, inv),
                (trans_hbm, trans),
                (near_hbm, near),
                (leaf_hbm, leaf),
            ]
        )
    ]
    for load in loads:
        load.start()
    half = lax.broadcasted_iota(jnp.int32, (16, 128), 1) // 64
    for i in range(UP):
        grams[i] = up_g[i]
    grams[UP] = root_g[...]
    factor(grams, up_inv, scratch, UP + 1)
    upper = lax.broadcasted_iota(jnp.int32, (64, 128), 0) <= lax.broadcasted_iota(
        jnp.int32, (64, 128), 1
    )
    root[...] = jnp.where(upper, scratch[2 * UP + 1], 0.0)[:, :64].T
    for load in loads:
        load.wait()

    for s, block in enumerate((rhs_lo, rhs, rhs_hi)):
        for j in range(8):
            a, b = dups(block[:, lanes(j)])
            points[16 * s + 2 * j] = a
            points[16 * s + 2 * j + 1] = b
    for k in range(4):
        size = 16 >> k
        for s, block in enumerate((xhat_lo, xhat, xhat_hi)):
            for j in range(size // 2):
                a, b = dups(block[PAIR_BASE[k] + j])
                at = 6 * PAIR_BASE[k] + size * s + 2 * j
                nodes[at] = a
                nodes[at + 1] = b

    lifts = []
    for b in range(UP):
        bi = bd(split(up_inv[b]))
        x = swap(nt(split(up_z[b]), bi))
        lifts.append(nn(split(nt(split(x), bd(split(up_s[b])))), bi))
    v = None
    for b in reversed(range(UP)):
        t = lifts[b]
        if v is not None:
            t = t + nt(split(v), bd(split(up_e[b])))
        v = jnp.where(half == level_at(b, grp, dev)[0], t, swap(t))

    held = [v]
    for k in reversed(range(4)):
        base = PAIR_BASE[k]
        start = 6 * base - first * (16 >> k)
        grown = []
        for i in range(8 >> k):
            p = base + i
            x = pick(
                nodes[start + far_partner[0, 2 * p]], nodes[start + far_partner[0, 2 * p + 1]]
            )
            y = nt(split(x), bd(split(couple[:, lanes(p)])))
            t = nn(split(y), bd(split(inv[p])))
            t = t + nt(split(held[i]), bd(split(trans[:, lanes(p)])))
            if k > 0:
                grown.extend(dups(t))
            else:
                far = nt(split(t), bd(split(leaf[:, lanes(i)])))
                cat = jnp.concatenate(
                    [
                        pick(points[16 + 2 * i + s], points[near_partner[2 * i + s] - first * 16])
                        for s in range(2)
                    ],
                    0,
                )
                d = jnp.concatenate([near[:, lanes(2 * i)], near[:, lanes(2 * i + 1)]], 0)
                o = nt(split(cat), split(d))
                product[:, lanes(i)] = pick(o[:16], o[16:]) + far
        held = grown


def shards(
    rhs,
    leaf_basis,
    near_blocks,
    near_partner,
    local_transfer,
    local_coupling,
    far_partner,
    dev_transfer,
    dev_coupling,
    grp_transfer,
    grp_coupling,
):
    vmem = pl.BlockSpec(memory_space=pltpu.VMEM)
    smem = pl.BlockSpec(memory_space=pltpu.SMEM)
    anywhere = pl.BlockSpec(memory_space=pl.ANY)

    def shape(*dims):
        return jax.ShapeDtypeStruct(dims, f32)

    def buffer(*dims):
        return pltpu.VMEM(dims, f32)

    inv, xhat, up_g, up_z, root_g, up_e, rhs_lo, rhs_hi, xhat_lo, xhat_hi = pl.pallas_call(
        kernel_climb,
        name="climb",
        out_shape=(
            shape(15, 64, 128),
            shape(15, 16, 128),
            shape(UP, 64, 128),
            shape(UP, 16, 128),
            shape(64, 128),
            shape(UP, 64, 128),
            shape(16, 1024),
            shape(16, 1024),
            shape(15, 16, 128),
            shape(15, 16, 128),
        ),
        in_specs=[anywhere] * 5,
        out_specs=(vmem,) * 10,
        scratch_shapes=[
            buffer(64, 1024),
            buffer(16, 1024),
            buffer(64, 1920),
            buffer(15, 64, 128),
            buffer(15, 16, 128),
            buffer(30, 64, 128),
            buffer(UP, 40, 128),
            buffer(UP, 40, 128),
            pltpu.SemaphoreType.DMA((UP,)),
            pltpu.SemaphoreType.DMA((UP,)),
            pltpu.SemaphoreType.DMA((4,)),
            pltpu.SemaphoreType.DMA((4,)),
            pltpu.SemaphoreType.DMA((UP + 3,)),
        ],
        compiler_params=pltpu.CompilerParams(collective_id=0, has_side_effects=True),
    )(leaf_basis, rhs, local_transfer, dev_transfer, grp_transfer)

    return pl.pallas_call(
        kernel_down,
        name="down",
        out_shape=(shape(16, 1024), shape(64, 64)),
        in_specs=[smem] * 2 + [vmem] * 4 + [anywhere] * 13,
        out_specs=(vmem,) * 2,
        scratch_shapes=[
            buffer(64, 1024),
            buffer(16, 1024),
            buffer(16, 1024),
            buffer(16, 1024),
            buffer(64, 2048),
            buffer(64, 1920),
            buffer(64, 1920),
            buffer(15, 64, 128),
            buffer(15, 16, 128),
            buffer(15, 16, 128),
            buffer(15, 16, 128),
            buffer(UP, 64, 128),
            buffer(UP + 1, 64, 128),
            buffer(UP + 1, 64, 128),
            buffer(2 * UP + 2, 64, 128),
            buffer(48, 16, 128),
            buffer(90, 16, 128),
            pltpu.SemaphoreType.DMA((UP + 11,)),
        ],
    )(
        near_partner,
        far_partner,
        up_g,
        up_z,
        root_g,
        up_e,
        dev_coupling,
        grp_coupling,
        leaf_basis,
        rhs,
        rhs_lo,
        rhs_hi,
        near_blocks,
        local_transfer,
        local_coupling,
        inv,
        xhat,
        xhat_lo,
        xhat_hi,
    )


def solution(mesh):
    return jax.shard_map(
        shards,
        mesh=mesh,
        in_specs=(
            P(None, ("grp", "dev")),
            P(None, ("grp", "dev")),
            P(None, ("grp", "dev")),
            P(("grp", "dev")),
            P(None, ("grp", "dev")),
            P(None, ("grp", "dev")),
            P(("grp", "dev"), None),
            P("grp", None, None),
            P("grp", None, None),
            P(),
            P(),
        ),
        out_specs=(P(None, ("grp", "dev")), P()),
        check_vma=False,
    )
```

time: 131 us -> 79.1 us (0.60)
  Pallas kernels: 127 us -> 76.7 us
  other arithmetic: 1.7 us -> 0 us
    pallas_call x3 -> x2, Pallas kernels: 127 us -> 76.7 us  [the longest x1 56.2 us: shards(): pl.pallas_call(kernel_climb, name='climb', out_shape=(shape(15, 64, 128),...]
where the time goes in v2:
time: 79.1 us; the launch traced here: 77.5 us
  Pallas kernels  76.7 us (97%)
  between operations  0.8 us (1%)
    pallas_call x1, Pallas kernels, shards(): pl.pallas_call(kernel_climb, name='climb', out_shape=(shape(15, 64, 128),...  56.2 us
    pallas_call x1, Pallas kernels, shards(): pl.pallas_call(kernel_down, name='down', out_shape=(shape(16, 1024), shap...  20.4 us

profile of v2, /device:TPU:6, one launch (start us, length us, event | category | flops | bytes accessed | tf_op | source)
XLA Modules:
  0.0 77.5 jit_solution(18278266637131140533)
XLA Ops:
  0.6 56.2 %climb.1 = (f32[15,64,128]{2,1,0:T(8,128)}, f32[15,16,128]{2,1,0:T(8,128)}, f32[9,64,128]{2,1,0:T(8,128)}, f32[9,16,128]{2,1,0:T(8,128)}, f32[64,128]{1,0:T(8,12...) custom-call(f32[64,1024]{1,0:T(8,128)} %leaf_hbm.3, ...), custom_call_target="tpu_custom_call" | custom-call | tf_op jit(solution)/shard_map/climb/pallas_call | solution.py:463
  56.9 20.4 %down.1 = (f32[16,1024]{1,0:T(8,128)}, f32[64,64]{1,0:T(8,128)}) custom-call(s32[16]{0:T(128)} %near_partner.1, s32[1,30]{1,0:T(1,128)} %far_partner.1, f32[9,64,128]{2,1,0:T(8,128)} %get-tuple-element.12.up_g, f32[9,16,128]{2,1,0:T(8,128)} %get-tuple-element.13.up_z, f32[64,128]{1,0:T(8,128)} %get-tuple-element.14.root_g, ...), custom_call_target="tpu_custom_call" | custom-call | tf_op jit(solution)/shard_map/down/pallas_call | solution.py:498

commit v3 on v2

v3 whole, which is shorter than its diff:
```python
import jax
import jax.numpy as jnp
from jax import lax
from jax.experimental import pallas as pl
from jax.experimental.pallas import tpu as pltpu
from jax.sharding import PartitionSpec as P

RANK = 64
NRHS = 16
LOC_PAIRS = 15
PAIR_BASE = (0, 8, 12, 14)
LOG_DEV = 5
LOG_GRP = 4
UP = LOG_DEV + LOG_GRP
ROUNDS = ((0,), (1, 2), (3, 4), (5, 6), (7, 8))
MESSAGES = 13
MESH = pl.DeviceIdType.MESH
f32 = jnp.float32
bf16 = jnp.bfloat16


def split(x):
    hi = x.astype(bf16)
    return hi, (x - hi.astype(f32)).astype(bf16)


def mm(a, b, ca, cb):
    return lax.dot_general(
        jnp.concatenate([a[0], a[1], a[0]], axis=ca),
        jnp.concatenate([b[0], b[0], b[1]], axis=cb),
        (((ca,), (cb,)), ((), ())),
        preferred_element_type=f32,
    )


def nn(a, b):
    return mm(a, b, 1, 0)


def nt(a, b):
    return mm(a, b, 1, 1)


def tn(a, b):
    return mm(a, b, 0, 0)


def left_of(rows):
    return lax.broadcasted_iota(jnp.int32, (rows, 128), 1) < 64


def swap(p):
    return pltpu.roll(p, 64, 1)


def fold(p):
    return p + swap(p)


def pick(a, b):
    return jnp.where(left_of(a.shape[0]), a, b)


def bd(pair):
    keep = left_of(64).astype(f32)
    left = keep.astype(bf16)
    right = (1.0 - keep).astype(bf16)
    return tuple(jnp.concatenate([x * left, x * right], axis=0) for x in pair)


def diag(c):
    return pick(c[:64], c[64:])


def dups(p):
    s = swap(p)
    return pick(p, s), pick(s, p)


def merge(g, z, e):
    es = split(e)
    lhs = tuple(jnp.concatenate([a, b], axis=0) for a, b in zip(bd(split(g)), split(z)))
    both = nn(lhs, bd(es))
    return fold(diag(tn(es, split(diag(both[:128]))))), fold(both[128:])


def across_rows(tile, row):
    at = jnp.full((8, 128), row, jnp.int32)
    return jnp.take_along_axis(tile, at, axis=0, mode="promise_in_bounds")


def stacked_blocks(wide, parts):
    lane = lax.broadcasted_iota(jnp.int32, (32, 128), 1) // 32
    keeps = [jnp.where(lane == q, 1.0, 0.0).astype(bf16) for q in range(4)]
    return tuple(
        jnp.concatenate([x[p : p + 32] * k for p, k in zip(parts, keeps)], axis=0)
        for x in split(wide)
    )


def eliminate(a, start):
    row = lax.broadcasted_iota(jnp.int32, (8, 128), 0)
    lane = lax.broadcasted_iota(jnp.int32, (8, 128), 1)
    out = [start[t] for t in range(4)]
    for j in range(0, 32, 2):
        h, js = j // 8, j % 8
        below = row > js + 1
        at = lane // 32 * 32 + j

        def across(tile, where):
            return jnp.take_along_axis(tile, where, axis=1, mode="promise_in_bounds")

        first = {t: across(a[t], at) for t in range(h, 4)}
        second = {t: across(a[t], at + 1) for t in range(h, 4)}
        yield
        i0 = lax.rsqrt(across_rows(first[h], js))
        q = across_rows(second[h], js) * i0
        i1 = lax.rsqrt(across_rows(second[h], js + 1) - q * q)
        top0 = across_rows(a[h], js) * i0
        top1 = (across_rows(a[h], js + 1) - q * top0) * i1
        eye0 = across_rows(out[h], js) * i0
        eye1 = (across_rows(out[h], js + 1) - q * eye0) * i1
        for t in range(h, 4):
            if t > h or js < 6:
                m0 = first[t] * i0
                m1 = (second[t] - m0 * q) * i1
                if t == h:
                    m0 = jnp.where(below, m0, 0.0)
                    m1 = jnp.where(below, m1, 0.0)
                a[t] = a[t] - m0 * top0 - m1 * top1
                out[t] = out[t] - m0 * eye0 - m1 * eye1
        out[h] = jnp.where(row == js, eye0, jnp.where(row == js + 1, eye1, out[h]))
        yield
    a[:] = out


def factor(grams, inverses, scratch, pairs):
    row = lax.broadcasted_iota(jnp.int32, (64, 128), 0)
    lane = lax.broadcasted_iota(jnp.int32, (64, 128), 1)
    left = lane < 64
    eye_left = jnp.where(row == lane, 1.0, 0.0)
    eye_right = jnp.where(row == lane - 64, 1.0, 0.0)
    for p in range(pairs):
        s = swap(grams[p])
        scratch[2 * p] = jnp.where(left, eye_left, s)
        scratch[2 * p + 1] = jnp.where(left, s, eye_right)
    nodes = 2 * pairs
    groups = []
    for g in range(0, nodes, 4):
        groups.append([g + q if g + q < nodes else g + q % 2 for q in range(4)])
    eyes = [
        jnp.where(
            lax.broadcasted_iota(jnp.int32, (8, 128), 0) + 8 * t
            == lax.broadcasted_iota(jnp.int32, (8, 128), 1) % 32,
            1.0,
            0.0,
        )
        for t in range(4)
    ]
    for lo in (0, 32):
        packs = []
        for members in groups:
            tiles = []
            for t in range(4):
                tile = None
                for q, n in enumerate(members):
                    shift = (32 * q - lo - (64 if n % 2 == 0 else 0)) % 128
                    x = scratch[n, lo + 8 * t : lo + 8 * t + 8, :]
                    x = pltpu.roll(x, shift, 1) if shift else x
                    tile = x if q == 0 else jnp.where(lane[:8] // 32 == q, x, tile)
                tiles.append(tile)
            packs.append(tiles)
        running = [eliminate(tiles, eyes) for tiles in packs]
        for _ in range(33):
            for run in running:
                next(run, None)
        for members, tiles in zip(groups, packs):
            rows = jnp.concatenate([scratch[n, lo : lo + 32, :] for n in members], axis=0)
            solved = nn(
                stacked_blocks(jnp.concatenate(tiles, axis=0), (0, 0, 0, 0)), split(rows)
            )
            if lo == 0:
                parts = [96 if n % 2 == 0 else 32 for n in members]
                change = nn(stacked_blocks(solved.T, parts), split(solved))
            for q, n in enumerate(members):
                if n == members[0] + q:
                    scratch[n, lo : lo + 32, :] = solved[32 * q : 32 * q + 32]
                    if lo == 0:
                        scratch[n, 32:64, :] -= change[32 * q : 32 * q + 32]
    for p in range(pairs):
        inverses[p] = jnp.where(left, scratch[2 * p], scratch[2 * p + 1])


def lanes(i):
    return slice(128 * i, 128 * i + 128)


def up_leaves(leaf, rhs, grams, zs):
    for j in range(8):
        u = split(leaf[:, lanes(j)])
        grams[j] = diag(tn(u, u))
        zs[j] = nn(split(rhs[:, lanes(j)]), bd(u))


def up_local(trans, grams, zs):
    for k in range(4):
        base = PAIR_BASE[k]
        held = None
        for i in range(8 >> k):
            g, z = merge(grams[base + i], zs[base + i], trans[:, lanes(base + i)])
            if k == 3:
                return g, z
            if i % 2 == 0:
                held = (g, z)
            else:
                grams[PAIR_BASE[k + 1] + i // 2] = pick(held[0], g)
                zs[PAIR_BASE[k + 1] + i // 2] = pick(held[1], z)


def pack(g, z):
    return pick(g[:32], g[32:]), pick(z[:8], z[8:])


def unpack(pg, pz):
    g0, g1 = dups(pg)
    z0, z1 = dups(pz)
    return jnp.concatenate([g0, g1], 0), jnp.concatenate([z0, z1], 0)


def spot(b, grp, dev):
    if b < LOG_DEV:
        return dev, b, 32
    return grp, b - LOG_DEV, 16


def bit_of(b, grp, dev):
    pos, lev, _ = spot(b, grp, dev)
    return lax.rem(pos // (1 << lev), 2)


def pair_block(b, grp, dev, dev_array, grp_array, other=False):
    pos, lev, size = spot(b, grp, dev)
    if other:
        pos = pos + (1 - 2 * bit_of(b + 1, grp, dev)) * (2 << lev)
    pair = size - (size >> lev) + pos // (2 << lev)
    at = pl.ds(pl.multiple_of(pair * 128, 128), 128)
    return dev_array.at[0, :, at] if b < LOG_DEV else grp_array.at[:, at]


def flipped(bits, grp, dev):
    for b in bits:
        lev = spot(b, grp, dev)[1]
        move = (1 - 2 * bit_of(b, grp, dev)) * (1 << lev)
        if b < LOG_DEV:
            dev = dev + move
        else:
            grp = grp + move
    return grp, dev


def kernel_climb(
    near_partner,
    far_partner,
    leaf_hbm,
    rhs_hbm,
    trans_hbm,
    near_hbm,
    couple_hbm,
    dev_trans,
    grp_trans,
    up_g,
    up_z,
    root_g,
    paths,
    lifts,
    base_out,
    rhs_lo,
    rhs_hi,
    xhat_lo,
    xhat_hi,
    leaf,
    rhs,
    trans,
    near,
    couple,
    inv,
    xhat,
    up_e,
    side_e,
    grams,
    zs,
    scratch,
    points,
    nodes,
    outgoing,
    incoming,
    send_sem,
    recv_sem,
    halo_send,
    halo_recv,
    load_sem,
):
    grp = lax.axis_index("grp")
    dev = lax.axis_index("dev")
    place = grp * 32 + dev
    first = place - 1
    after = lax.rem(place + 1, 512)
    before = lax.rem(place + 511, 512)
    right = (after // 32, lax.rem(after, 32))
    left = (before // 32, lax.rem(before, 32))
    barrier = pltpu.get_barrier_semaphore()
    peers = []
    for bits in ROUNDS:
        flips = [bits] if len(bits) == 1 else [bits[:1], bits[1:], bits]
        peers.append([flipped(f, grp, dev) for f in flips])
    greeted = [p for group in peers for p in group] + [left, right]
    for peer in greeted:
        pl.semaphore_signal(barrier, inc=1, device_id=peer, device_id_type=MESH)

    wanted = [(leaf_hbm, leaf), (rhs_hbm, rhs), (trans_hbm, trans)]
    for b in range(UP):
        wanted.append((pair_block(b, grp, dev, dev_trans, grp_trans), up_e.at[b]))
    for i, bits in enumerate(ROUNDS[1:]):
        wanted.append(
            (pair_block(bits[0], grp, dev, dev_trans, grp_trans, True), side_e.at[i])
        )
    wanted.extend([(near_hbm, near), (couple_hbm, couple)])
    loads = [
        pltpu.make_async_copy(s, d, load_sem.at[i]) for i, (s, d) in enumerate(wanted)
    ]
    for load in loads:
        load.start()

    def copy(src, dst, s, r, peer):
        return pltpu.make_async_remote_copy(
            src_ref=src,
            dst_ref=dst,
            send_sem=s,
            recv_sem=r,
            device_id=peer,
            device_id_type=MESH,
        )

    halos = [
        copy(rhs, rhs_lo, halo_send.at[0], halo_recv.at[0], right),
        copy(rhs, rhs_hi, halo_send.at[1], halo_recv.at[1], left),
        copy(xhat, xhat_lo, halo_send.at[2], halo_recv.at[2], right),
        copy(xhat, xhat_hi, halo_send.at[3], halo_recv.at[3], left),
    ]
    half = lax.broadcasted_iota(jnp.int32, (64, 128), 1) // 64
    mine = [half == bit_of(b, grp, dev) for b in range(UP)]

    def factor_local():
        factor(grams, inv, scratch, LOC_PAIRS)
        for i in range(LOC_PAIRS):
            xhat[i] = nt(split(zs[i]), bd(split(inv[i])))
        halos[2].start()
        halos[3].start()

    def near_field():
        halos[0].wait()
        halos[1].wait()
        loads[-2].wait()
        for s, block in enumerate((rhs_lo, rhs, rhs_hi)):
            for j in range(8):
                a, b = dups(block[:, lanes(j)])
                points[16 * s + 2 * j] = a
                points[16 * s + 2 * j + 1] = b
        for i in range(8):
            cat = jnp.concatenate(
                [
                    pick(points[16 + 2 * i + s], points[jnp.clip(near_partner[2 * i + s] - first * 16, 0, 47)])
                    for s in range(2)
                ],
                0,
            )
            d = jnp.concatenate([near[:, lanes(2 * i)], near[:, lanes(2 * i + 1)]], 0)
            o = nt(split(cat), split(d))
            base_out[:, lanes(i)] = pick(o[:16], o[16:])

    def local_lifts():
        halos[2].wait()
        halos[3].wait()
        loads[-1].wait()
        for k in range(4):
            size = 16 >> k
            base = PAIR_BASE[k]
            for s, block in enumerate((xhat_lo, xhat, xhat_hi)):
                for j in range(size // 2):
                    a, b = dups(block[base + j])
                    at = 6 * base + size * s + 2 * j
                    nodes[at] = a
                    nodes[at + 1] = b
            for i in range(8 >> k):
                p = base + i
                x = pick(
                    nodes[6 * base + jnp.clip(far_partner[0, 2 * p] - first * size, 0, 3 * size - 1)],
                    nodes[6 * base + jnp.clip(far_partner[0, 2 * p + 1] - first * size, 0, 3 * size - 1)],
                )
                y = nt(split(x), bd(split(couple[:, lanes(p)])))
                lifts[p] = nn(split(y), bd(split(inv[p])))

    def extend_paths(levels):
        for b in levels:
            e = up_e[b]
            if b > 0:
                e = nn(split(paths[b - 1]), bd(split(e)))
            paths[b] = jnp.where(mine[b], e, swap(e))

    loads[0].wait()
    loads[1].wait()
    up_leaves(leaf, rhs, grams, zs)
    loads[2].wait()
    own_g, own_z = up_local(trans, grams, zs)
    for load in loads[3:-2]:
        load.wait()
    pl.semaphore_wait(barrier, len(greeted))
    slot = 0
    for r, bits in enumerate(ROUNDS):
        pg, pz = pack(own_g, own_z)
        outgoing[r, 0:32, :] = pg
        outgoing[r, 32:40, :] = pz
        steps = []
        for i, peer in enumerate(peers[r]):
            at = slot + i
            steps.append(
                copy(outgoing.at[r], incoming.at[at], send_sem.at[at], recv_sem.at[at], peer)
            )
        for step in steps:
            step.start()
        if r == 0:
            halos[0].start()
            halos[1].start()
            extend_paths((0,))
        elif r == 1:
            extend_paths((1, 2))
        elif r == 2:
            factor_local()
            extend_paths((3, 4))
        elif r == 3:
            near_field()
            extend_paths((5, 6, 7))
        else:
            local_lifts()
        for step in steps:
            step.wait()
        b = bits[0]
        got = [
            unpack(incoming[slot + i, 0:32, :], incoming[slot + i, 32:40, :])
            for i in range(len(steps))
        ]
        slot += len(steps)
        g = jnp.where(mine[b], own_g, got[0][0])
        z = jnp.where(mine[b][:16], own_z, got[0][1])
        up_g[b] = g
        up_z[b] = z
        own_g, own_z = merge(g, z, up_e[b])
        if len(bits) == 2:
            g = jnp.where(mine[b], got[1][0], got[2][0])
            z = jnp.where(mine[b][:16], got[1][1], got[2][1])
            side_g, side_z = merge(g, z, side_e[r - 1])
            g = jnp.where(mine[b + 1], own_g, side_g)
            z = jnp.where(mine[b + 1][:16], own_z, side_z)
            up_g[b + 1] = g
            up_z[b + 1] = z
            own_g, own_z = merge(g, z, up_e[b + 1])
    root_g[...] = own_g


def kernel_down(
    up_g,
    up_z,
    root_g,
    paths,
    lifts,
    base_in,
    dev_couple,
    grp_couple,
    leaf_hbm,
    trans_hbm,
    product,
    root,
    leaf,
    trans,
    up_s,
    grams,
    up_inv,
    scratch,
    load_sem,
):
    grp = lax.axis_index("grp")
    dev = lax.axis_index("dev")
    wanted = [
        (pair_block(b, grp, dev, dev_couple, grp_couple), up_s.at[b]) for b in range(UP)
    ]
    wanted.extend([(trans_hbm, trans), (leaf_hbm, leaf)])
    loads = [
        pltpu.make_async_copy(s, d, load_sem.at[i]) for i, (s, d) in enumerate(wanted)
    ]
    for load in loads:
        load.start()
    half = lax.broadcasted_iota(jnp.int32, (16, 128), 1) // 64
    for i in range(UP):
        grams[i] = up_g[i]
    grams[UP] = root_g[...]
    factor(grams, up_inv, scratch, UP + 1)
    upper = lax.broadcasted_iota(jnp.int32, (64, 128), 0) <= lax.broadcasted_iota(
        jnp.int32, (64, 128), 1
    )
    root[...] = jnp.where(upper, scratch[2 * UP + 1], 0.0)[:, :64].T
    for load in loads:
        load.wait()

    v = None
    for b in range(UP):
        bi = bd(split(up_inv[b]))
        x = swap(nt(split(up_z[b]), bi))
        t = nn(split(nt(split(x), bd(split(up_s[b])))), bi)
        t = jnp.where(half == bit_of(b, grp, dev), t, swap(t))
        if b == 0:
            v = t
        else:
            path = tuple(jnp.concatenate([x, x], axis=0) for x in split(paths[b - 1]))
            v = v + nt(split(jnp.where(half == 0, t, 0.0)), path)

    held = [v]
    for k in reversed(range(4)):
        grown = []
        for i in range(8 >> k):
            p = PAIR_BASE[k] + i
            t = lifts[p] + nt(split(held[i]), bd(split(trans[:, lanes(p)])))
            if k > 0:
                grown.extend(dups(t))
            else:
                far = nt(split(t), bd(split(leaf[:, lanes(i)])))
                product[:, lanes(i)] = base_in[:, lanes(i)] + far
        held = grown


def shards(
    rhs,
    leaf_basis,
    near_blocks,
    near_partner,
    local_transfer,
    local_coupling,
    far_partner,
    dev_transfer,
    dev_coupling,
    grp_transfer,
    grp_coupling,
):
    vmem = pl.BlockSpec(memory_space=pltpu.VMEM)
    smem = pl.BlockSpec(memory_space=pltpu.SMEM)
    anywhere = pl.BlockSpec(memory_space=pl.ANY)

    def shape(*dims):
        return jax.ShapeDtypeStruct(dims, f32)

    def buffer(*dims):
        return pltpu.VMEM(dims, f32)

    handed = pl.pallas_call(
        kernel_climb,
        name="climb",
        out_shape=(
            shape(UP, 64, 128),
            shape(UP, 16, 128),
            shape(64, 128),
            shape(UP - 1, 64, 128),
            shape(15, 16, 128),
            shape(16, 1024),
        ),
        in_specs=[smem] * 2 + [anywhere] * 7,
        out_specs=(vmem,) * 6,
        scratch_shapes=[
            buffer(16, 1024),
            buffer(16, 1024),
            buffer(15, 16, 128),
            buffer(15, 16, 128),
            buffer(64, 1024),
            buffer(16, 1024),
            buffer(64, 1920),
            buffer(64, 2048),
            buffer(64, 1920),
            buffer(15, 64, 128),
            buffer(15, 16, 128),
            buffer(UP, 64, 128),
            buffer(len(ROUNDS) - 1, 64, 128),
            buffer(15, 64, 128),
            buffer(15, 16, 128),
            buffer(30, 64, 128),
            buffer(48, 16, 128),
            buffer(90, 16, 128),
            buffer(len(ROUNDS), 40, 128),
            buffer(MESSAGES, 40, 128),
            pltpu.SemaphoreType.DMA((MESSAGES,)),
            pltpu.SemaphoreType.DMA((MESSAGES,)),
            pltpu.SemaphoreType.DMA((4,)),
            pltpu.SemaphoreType.DMA((4,)),
            pltpu.SemaphoreType.DMA((UP + len(ROUNDS) + 4,)),
        ],
        compiler_params=pltpu.CompilerParams(collective_id=0, has_side_effects=True),
    )(
        near_partner,
        far_partner,
        leaf_basis,
        rhs,
        local_transfer,
        near_blocks,
        local_coupling,
        dev_transfer,
        grp_transfer,
    )

    return pl.pallas_call(
        kernel_down,
        name="down",
        out_shape=(shape(16, 1024), shape(64, 64)),
        in_specs=[vmem] * 6 + [anywhere] * 4,
        out_specs=(vmem,) * 2,
        scratch_shapes=[
            buffer(64, 1024),
            buffer(64, 1920),
            buffer(UP, 64, 128),
            buffer(UP + 1, 64, 128),
            buffer(UP + 1, 64, 128),
            buffer(2 * UP + 2, 64, 128),
            pltpu.SemaphoreType.DMA((UP + 2,)),
        ],
    )(*handed, dev_coupling, grp_coupling, leaf_basis, local_transfer)


def solution(mesh):
    return jax.shard_map(
        shards,
        mesh=mesh,
        in_specs=(
            P(None, ("grp", "dev")),
            P(None, ("grp", "dev")),
            P(None, ("grp", "dev")),
            P(("grp", "dev")),
            P(None, ("grp", "dev")),
            P(None, ("grp", "dev")),
            P(("grp", "dev"), None),
            P("grp", None, None),
            P("grp", None, None),
            P(),
            P(),
        ),
        out_specs=(P(None, ("grp", "dev")), P()),
        check_vma=False,
    )
```

time: 79.1 us -> 65.3 us (0.83)
  Pallas kernels: 76.7 us -> 63.6 us
    pallas_call x1, Pallas kernels: 20.4 us -> 13.9 us  [shards(): pl.pallas_call(kernel_down, name='down', out_shape=(shape(16, 1024), shap...]
    pallas_call x1, Pallas kernels: 56.2 us -> 49.7 us  [shards(): pl.pallas_call(kernel_climb, name='climb', out_shape=(shape(UP, 64, 128),...]
where the time goes in v3:
time: 65.3 us; the launch traced here: 64.4 us
  Pallas kernels  63.6 us (97%)
  between operations  0.8 us (1%)
    pallas_call x1, Pallas kernels, shards(): pl.pallas_call(kernel_climb, name='climb', out_shape=(shape(UP, 64, 128),...  49.7 us
    pallas_call x1, Pallas kernels, shards(): pl.pallas_call(kernel_down, name='down', out_shape=(shape(16, 1024), shap...  13.9 us

profile of v3, /device:TPU:6, one launch (start us, length us, event | category | flops | bytes accessed | tf_op | source)
XLA Modules:
  0.0 64.4 jit_solution(9671127152599642209)
XLA Ops:
  0.6 49.7 %climb.1 = (f32[9,64,128]{2,1,0:T(8,128)}, f32[9,16,128]{2,1,0:T(8,128)}, f32[64,128]{1,0:T(8,128)}, f32[8,64,128]{2,1,0:T(8,128)}, f32[15,16,128]{2,1,0:T(8,128)}, /*index=5*/f32[16,1024]{1,0:T(8,128)}) custom-call(s32[16]{0:T(128)} %near_partner.1, s32[1,30]{1,0:T(1,128)} %far_partner.1, f32[64,1024]{1,0:T(8,128)} %leaf_hbm.3, f32[16,1024]{1,0:T(8,128)} %rhs_hbm.1, ...), custom_call_target="tpu_custom_call" | custom-call | tf_op jit(solution)/shard_map/climb/pallas_call | solution.py:563
  50.3 13.9 %down.1 = (f32[16,1024]{1,0:T(8,128)}, f32[64,64]{1,0:T(8,128)}) custom-call(f32[9,64,128]{2,1,0:T(8,128)} %get-tuple-element.8.up_g, f32[9,16,128]{2,1,0:T(8,128)} %get-tuple-element.9.up_z, f32[64,128]{1,0:T(8,128)} %get-tuple-element.10.root_g, f32[8,64,128]{2,1,0:T(8,128)} %get-tuple-element.11.paths, f32[15,16,128]{2,1,0:T(8,128)} %get-tuple-element.12.lifts, ...), custom_call_target="tpu_custom_call" | custom-call | tf_op jit(solution)/shard_map/down/pallas_call | solution.py:616

commit v4 on v3

--- a/solution.py
+++ b/solution.py
@@ -79,9 +79,8 @@
 
 def merge(g, z, e):
     es = split(e)
-    lhs = tuple(jnp.concatenate([a, b], axis=0) for a, b in zip(bd(split(g)), split(z)))
-    both = nn(lhs, bd(es))
-    return fold(diag(tn(es, split(diag(both[:128]))))), fold(both[128:])
+    both = nn(split(jnp.concatenate([g, z], axis=0)), bd(es))
+    return fold(diag(tn(es, split(both[:64])))), fold(both[64:])
 
 
 def across_rows(tile, row):
@@ -268,9 +267,14 @@
     couple_hbm,
     dev_trans,
     grp_trans,
+    dev_couple,
+    grp_couple,
+    product,
+    root,
     up_g,
     up_z,
-    root_g,
+    up_s,
+    up_inv,
     paths,
     lifts,
     base_out,
@@ -324,6 +328,8 @@
         wanted.append(
             (pair_block(bits[0], grp, dev, dev_trans, grp_trans, True), side_e.at[i])
         )
+    for b in range(UP):
+        wanted.append((pair_block(b, grp, dev, dev_couple, grp_couple), up_s.at[b]))
     wanted.extend([(near_hbm, near), (couple_hbm, couple)])
     loads = [
         pltpu.make_async_copy(s, d, load_sem.at[i]) for i, (s, d) in enumerate(wanted)
@@ -464,64 +470,24 @@
             up_g[b + 1] = g
             up_z[b + 1] = z
             own_g, own_z = merge(g, z, up_e[b + 1])
-    root_g[...] = own_g
-
-
-def kernel_down(
-    up_g,
-    up_z,
-    root_g,
-    paths,
-    lifts,
-    base_in,
-    dev_couple,
-    grp_couple,
-    leaf_hbm,
-    trans_hbm,
-    product,
-    root,
-    leaf,
-    trans,
-    up_s,
-    grams,
-    up_inv,
-    scratch,
-    load_sem,
-):
-    grp = lax.axis_index("grp")
-    dev = lax.axis_index("dev")
-    wanted = [
-        (pair_block(b, grp, dev, dev_couple, grp_couple), up_s.at[b]) for b in range(UP)
-    ]
-    wanted.extend([(trans_hbm, trans), (leaf_hbm, leaf)])
-    loads = [
-        pltpu.make_async_copy(s, d, load_sem.at[i]) for i, (s, d) in enumerate(wanted)
-    ]
-    for load in loads:
-        load.start()
-    half = lax.broadcasted_iota(jnp.int32, (16, 128), 1) // 64
-    for i in range(UP):
-        grams[i] = up_g[i]
-    grams[UP] = root_g[...]
-    factor(grams, up_inv, scratch, UP + 1)
+    up_g[UP] = own_g
+    side = lax.broadcasted_iota(jnp.int32, (16, 128), 1) // 64
+    factor(up_g, up_inv, scratch, UP + 1)
     upper = lax.broadcasted_iota(jnp.int32, (64, 128), 0) <= lax.broadcasted_iota(
         jnp.int32, (64, 128), 1
     )
     root[...] = jnp.where(upper, scratch[2 * UP + 1], 0.0)[:, :64].T
-    for load in loads:
-        load.wait()
-
     v = None
     for b in range(UP):
         bi = bd(split(up_inv[b]))
         x = swap(nt(split(up_z[b]), bi))
         t = nn(split(nt(split(x), bd(split(up_s[b])))), bi)
-        t = jnp.where(half == bit_of(b, grp, dev), t, swap(t))
+        t = jnp.where(side == bit_of(b, grp, dev), t, swap(t))
         if b == 0:
             v = t
         else:
             path = tuple(jnp.concatenate([x, x], axis=0) for x in split(paths[b - 1]))
-            v = v + nt(split(jnp.where(half == 0, t, 0.0)), path)
+            v = v + nt(split(jnp.where(side == 0, t, 0.0)), path)
 
     held = [v]
     for k in reversed(range(4)):
@@ -533,7 +499,7 @@
                 grown.extend(dups(t))
             else:
                 far = nt(split(t), bd(split(leaf[:, lanes(i)])))
-                product[:, lanes(i)] = base_in[:, lanes(i)] + far
+                product[:, lanes(i)] = base_out[:, lanes(i)] + far
         held = grown
 
 
@@ -560,20 +526,20 @@
     def buffer(*dims):
         return pltpu.VMEM(dims, f32)
 
-    handed = pl.pallas_call(
+    return pl.pallas_call(
         kernel_climb,
         name="climb",
-        out_shape=(
-            shape(UP, 64, 128),
-            shape(UP, 16, 128),
-            shape(64, 128),
-            shape(UP - 1, 64, 128),
-            shape(15, 16, 128),
-            shape(16, 1024),
-        ),
-        in_specs=[smem] * 2 + [anywhere] * 7,
-        out_specs=(vmem,) * 6,
+        out_shape=(shape(16, 1024), shape(64, 64)),
+        in_specs=[smem] * 2 + [anywhere] * 9,
+        out_specs=(vmem,) * 2,
         scratch_shapes=[
+            buffer(UP + 1, 64, 128),
+            buffer(UP, 16, 128),
+            buffer(UP, 64, 128),
+            buffer(UP + 1, 64, 128),
+            buffer(UP - 1, 64, 128),
+            buffer(15, 16, 128),
+            buffer(16, 1024),
             buffer(16, 1024),
             buffer(16, 1024),
             buffer(15, 16, 128),
@@ -598,7 +564,7 @@
             pltpu.SemaphoreType.DMA((MESSAGES,)),
             pltpu.SemaphoreType.DMA((4,)),
             pltpu.SemaphoreType.DMA((4,)),
-            pltpu.SemaphoreType.DMA((UP + len(ROUNDS) + 4,)),
+            pltpu.SemaphoreType.DMA((2 * UP + len(ROUNDS) + 4,)),
         ],
         compiler_params=pltpu.CompilerParams(collective_id=0, has_side_effects=True),
     )(
@@ -611,24 +577,9 @@
         local_coupling,
         dev_transfer,
         grp_transfer,
+        dev_coupling,
+        grp_coupling,
     )
-
-    return pl.pallas_call(
-        kernel_down,
-        name="down",
-        out_shape=(shape(16, 1024), shape(64, 64)),
-        in_specs=[vmem] * 6 + [anywhere] * 4,
-        out_specs=(vmem,) * 2,
-        scratch_shapes=[
-            buffer(64, 1024),
-            buffer(64, 1920),
-            buffer(UP, 64, 128),
-            buffer(UP + 1, 64, 128),
-            buffer(UP + 1, 64, 128),
-            buffer(2 * UP + 2, 64, 128),
-            pltpu.SemaphoreType.DMA((UP + 2,)),
-        ],
-    )(*handed, dev_coupling, grp_coupling, leaf_basis, local_transfer)
 
 
 def solution(mesh):

time: 65.3 us -> 63.6 us (0.974)
  Pallas kernels: 63.6 us -> 59.9 us
  local copies, waits for them, and re-layouts: 0 us -> 2.1 us
    pallas_call x2 -> x1, Pallas kernels: 63.6 us -> 59.9 us  [shards(): pl.pallas_call(kernel_climb, name='climb', out_shape=(shape(16, 1024), sh...]
    unnamed x0 -> x4, local copies, waits for them, and re-layouts: none -> 2.1 us
where the time goes in v4:
time: 63.6 us; the launch traced here: 62.6 us
  Pallas kernels  59.9 us (94%)
  local copies, waits for them, and re-layouts  2.1 us (3%)
  between operations  0.65 us (1%)
    pallas_call x1, Pallas kernels, shards(): pl.pallas_call(kernel_climb, name='climb', out_shape=(shape(16, 1024), sh...  59.9 us
    unnamed x4, local copies, waits for them, and re-layouts  2.1 us

profile of v4, /device:TPU:6, one launch (start us, length us, event | category | flops | bytes accessed | tf_op | source)
XLA Modules:
  0.0 62.6 jit_solution(15606481870929326834)
XLA Ops:
  0.6 59.9 %climb.1 = (f32[16,1024]{1,0:T(8,128)}, f32[64,64]{1,0:T(8,128)}) custom-call(s32[16]{0:T(128)} %near_partner.1, s32[1,30]{1,0:T(1,128)} %far_partner.1, f32[64,1024]{1,0:T(8,128)} %leaf_hbm.1, f32[16,1024]{1,0:T(8,128)} %rhs_hbm.1, f32[64,1920]{1,0:T(8,128)} %trans_hbm.1, f32[64,2048]{1,0:T(8,128)} %near_hbm.1, f32[64,1920]{1,0:T(8,128)} %couple_hbm.1, ...), custom_call_target="tpu_custom_call" | custom-call | tf_op jit(solution)/shard_map/climb/pallas_call | solution.py:529
  60.5 0.0 copy-start
  60.6 1.5 %copy.15 = f32[16,1024]{1,0:T(8,128)} copy(f32[16,1024]{1,0:T(8,128)} %get-tuple-element.4) | data formatting | bytes 131072
  62.0 0.0 copy-done
  62.0 0.6 copy.16
Async XLA Ops:
  60.5 1.5 %copy-start = (f32[64,64]{1,0:T(8,128)S(1)}, f32[64,64]{1,0:T(8,128)}, u32[]{:S(2)}) copy-start(f32[64,64]{1,0:T(8,128)} %get-tuple-element.5) | copy-start | bytes 49156
